TPU v7x, 128 devices: a whole 4x4x4 slice. The times are simulated.
128 devices in a mesh: row: 2 (over core), blk: 64 (over x, z, y).
Axes of the slice: x: 4, y: 4, z: 4, core: 2. Of those that a mesh axis runs over, the one named last changes fastest.
Arguments:
- flow_state: float32 [2, 64, 6, 16, 64, 256], P('row', 'blk'), may hold values from -6 to 6
- forcing: float32 [2, 64, 6, 16, 64, 256], P('row', 'blk'), may hold values from -6 to 6
- stiffness: float32 [2, 64, 16, 64, 256], P('row', 'blk'), may hold values from 7 to 14
- advection: float32 [2, 64, 6, 6], P('row', 'blk'), may hold values from -4 to 4
- line_inverse: float32 [2, 64, 96, 96], P('row', 'blk')
- margin_rows: int32 [2, 64, 64, 4], P('row', 'blk'), may hold values from 0 to 67, as said below
- margin_weights: float32 [2, 64, 64, 4], P('row', 'blk'), may hold values from 0 to 1, as said below
- partner_bit: int32 [2, 64], P('row', 'blk'), may hold values from 0 to 2, as said below
- turn_code: int32 [2, 64], P('row', 'blk'), may hold values from 0 to 3, as said below
Outputs:
- final_state: float32 [2, 64, 6, 16, 64, 256], P('row', 'blk')
Inputs may be any that keep to these rules, and one draw needn't show every extreme that they name: Within a blade row, blocks 8g to 8g+7 share one value, so that b and b XOR 2**partner_bit[r,b] name each other. `turn_code`: A block and its face partner carry the same code. `margin_rows`: row j of a block reads window rows j to j + 4 only. `margin_weights`: the first 1 to 4 slots of a row carry positive weights summing to one, the others zero.
All inputs are finite; a program needn't handle non-finite values.
Results may differ from a plain program's by a relative error of at most 0.0001.
Values sent between devices are 32-bit elements; how exact they have to be, the bound alone decides.
No kernel may reach another device: no remote copies, remote signals or barrier semaphores. Data moves between devices by JAX's collectives and lax.ppermute only.
A program may use at most 128 MiB of HBM per device.

v0:
```python
import jax
import jax.numpy as jnp
from jax import lax
from jax.sharding import PartitionSpec as P

HW = 2
SWEEPS = 3


def padded(cells, sides, width):
    for axis, dim in sides:
        count = lax.axis_size(axis)
        head = lax.slice_in_dim(cells, 0, width, axis=dim)
        tail = lax.slice_in_dim(cells, cells.shape[dim] - width, cells.shape[dim], axis=dim)
        cells = jnp.concatenate(
            [
                lax.ppermute(tail, axis, [(i, (i + 1) % count) for i in range(count)]),
                cells,
                lax.ppermute(head, axis, [((i + 1) % count, i) for i in range(count)]),
            ],
            axis=dim,
        )
    return cells


def from_partner(value, axis, stride):
    return lax.ppermute(value, axis, [(i, i ^ 1 << stride) for i in range(lax.axis_size(axis))])


def orient(surface, turn_code):
    flipped = jnp.flip(surface, -2)
    first = jnp.where(turn_code % 2 == 1, flipped, surface)
    second = jnp.flip(first, -1)
    return jnp.where(turn_code // 2 == 1, second, first)


def blend_matrix(rows_used, weights, extent):
    onehot = (rows_used[..., None] == jnp.arange(extent, dtype=jnp.int32)).astype(jnp.float32)
    return jnp.sum(weights[..., None] * onehot, axis=-2)


def operate(
    field, forcing, stiffness, advection, inlet_ghost, outlet_ghost, lower_ghost, upper_ghost
):
    along_i = jnp.concatenate(
        [inlet_ghost[:, None, :, :], field, outlet_ghost[:, None, :, :]], axis=1
    )
    along_j = jnp.concatenate(
        [lower_ghost[:, :, None, :], field, upper_ghost[:, :, None, :]], axis=2
    )
    walls = jnp.zeros_like(field[..., :1])
    along_k = jnp.concatenate([walls, field, walls], axis=3)
    neighbours = along_i[:, 2:] + along_i[:, :-2]
    neighbours = neighbours + along_j[:, :, 2:] + along_j[:, :, :-2]
    neighbours = neighbours + along_k[..., 2:] + along_k[..., :-2]
    stretch = along_i[:, 2:] - along_i[:, :-2]
    carried = 0.5 * jnp.einsum("vw,wijk->vijk", advection, stretch, precision=lax.Precision.HIGHEST)
    return forcing - (stiffness[None] * field - neighbours + carried)


def body(
    flow_state,
    forcing,
    stiffness,
    advection,
    line_inverse,
    margin_rows,
    margin_weights,
    partner_bit,
    turn_code,
):
    field = flow_state[0, 0]
    source_term = forcing[0, 0]
    diagonal = stiffness[0, 0]
    jacobian = advection[0, 0]
    inverse = line_inverse[0, 0]
    variables, line_cells, pitch_rows, span_cells = field.shape
    blend = blend_matrix(margin_rows[0, 0], margin_weights[0, 0], pitch_rows + 2 * HW)
    rotor = lax.axis_index("row") == 0
    pair_level = partner_bit[0, 0]
    rotation = turn_code[0, 0]
    for sweep in range(SWEEPS):
        boundary = jnp.where(rotor, field[:, line_cells - 1], field[:, 0])
        own_window = padded(boundary, (("blk", 1),), HW)
        window = from_partner(own_window, "row", 0)
        ghosts = jnp.einsum("jm,vmk->vjk", blend, window, precision=lax.Precision.HIGHEST)
        inlet_ghost = jnp.where(rotor, field[:, 0], ghosts)
        outlet_ghost = jnp.where(rotor, ghosts, field[:, line_cells - 1])
        faces = jnp.stack([field[:, :, 0, :], field[:, :, pitch_rows - 1, :]])
        received = jnp.zeros_like(faces)
        for bit_index in range(3):
            swapped = from_partner(faces, "blk", bit_index)
            received = jnp.where(pair_level == bit_index, swapped, received)
        lower_ghost = orient(received[1], rotation)
        upper_ghost = orient(received[0], rotation)
        residue = operate(
            field,
            source_term,
            diagonal,
            jacobian,
            inlet_ghost,
            outlet_ghost,
            lower_ghost,
            upper_ghost,
        )
        flat = residue.reshape((variables * line_cells, pitch_rows * span_cells))
        change = jnp.dot(inverse, flat, precision=lax.Precision.HIGHEST)
        field = field + change.reshape(field.shape)
    return field[None, None]


def solution(mesh):
    return jax.shard_map(
        body,
        mesh=mesh,
        in_specs=(
            P("row", "blk", None, None, None, None),
            P("row", "blk", None, None, None, None),
            P("row", "blk", None, None, None),
            P("row", "blk", None, None),
            P("row", "blk", None, None),
            P("row", "blk", None, None),
            P("row", "blk", None, None),
            P("row", "blk"),
            P("row", "blk"),
        ),
        out_specs=P("row", "blk", None, None, None, None),
        check_vma=False,
    )
```

profile of v0, /device:TPU:1, one launch (start us, length us, event | category | flops | bytes accessed | tf_op | source)
XLA Modules:
  0.0 222.6 jit_solution(14636061826098508037)
XLA Ops:
  0.0 3.5 %copy.486 = f32[1,1,6,16,64,256]{5,4,2,3,1,0:T(8,128)S(1)} copy(f32[1,1,6,16,64,256]{5,4,3,2,1,0:T(8,128)} %param.9) | data formatting | bytes 12582912 | tf_op args[0]
  14.2 6.9 %collective-permute-start.1 = (f32[6,2,256]{2,1,0:T(2,128)S(1)}, f32[6,2,256]{2,1,0:T(2,128)S(1)}, u32[]{:S(2)}, u32[]{:S(2)}) collective-permute-start(f32[6,2,256]{2,1,0:T(2,128)S(1)} %get-tuple-element.22), channel_id=1, source_target_pairs={{1,0},{2,1},{3,2},{4,3},{5,4},{6,5},{7,6},{8,7},{9,8},{10,9},{11,1... | collective-permute-start | bytes 36872 | tf_op jit(solution)/shard_map/ppermute | solution.py:19
  22.6 3.0 %collective-permute-start.2 = (f32[6,68,256]{2,1,0:T(8,128)S(1)}, f32[6,68,256]{2,1,0:T(8,128)S(1)}, u32[]{:S(2)}, u32[]{:S(2)}) collective-permute-start(f32[6,68,256]{2,1,0:T(8,128)S(1)} %pad_maximum_fusion.12), channel_id=1, source_target_pairs={{0,64},{64,0},{1,65},{65,1},{2,66},{66,2},{3,67},{67,3},{4,68},{68... | collective-permute-start | bytes 1253384 | tf_op jit(solution)/shard_map/ppermute | solution.py:27
  30.2 5.1 %fusion.27 = f32[6,16,64,256]{3,2,0,1:T(8,128)S(1)} fusion(f32[6,1,64,256]{3,2,0,1:T(8,128)S(1)} %get-tuple-element.10, f32[6,16,64,256]{3,2,0,1:T(8,128)} %bitcast.213, f32[6,1,64,256]{3,2,0,1:T(8,128)S(1)} %get-tuple-element.9), kind=kLoop, calls=%fused_computation.52 | loop fusion | flops 4718592 | bytes 13369344 | tf_op jit(solution)/shard_map/sub | solution.py:56
  35.4 12.6 %fusion.4 = f32[16,64,256,6]{2,3,1,0:T(8,128)} fusion(f32[6,16,64,256]{3,2,0,1:T(8,128)S(1)} %fusion.27, f32[1,1,6,6]{3,1,2,0:T(1,128)S(1)} %copy-done.10), kind=kOutput, calls=%fused_computation.10 | convolution fusion | flops 113246208 | bytes 12583056 | tf_op jit(solution)/shard_map/vw,wijk->vijk/dot_general | solution.py:57
  48.0 12.1 %fusion.10 = f32[6,16,64,256]{3,2,0,1:T(8,128)S(1)} fusion(f32[6,16,64,256]{3,2,0,1:T(8,128)S(1)} %bitcast.216, f32[6,16,1,256]{3,2,0,1:T(1,128)} %copy.415, f32[6,16,1,256]{3,2,0,1:T(1,128)} %copy.414, f32[16,64,256,6]{2,3,1,0:T(8,128)} %fusion.4, f32[1,1,6,16,64,256]{5,4,3,2,1,0:T(8,128)S(1)} %bitcast.220, f32[6,1,64,256]{3,2,0,1:T(8,128)} %copy-done.7, ...), kind=kLoop, calls=%fused_computation.16 | loop fusion | flops 22020096 | bytes 27197440 | tf_op jit(solution)/shard_map/sub | solution.py:58
  60.6 4.4 %copy.437 = f32[12,8,64,256]{3,1,2,0:T(8,128)S(1)} copy(f32[12,8,64,256]{3,2,1,0:T(8,128)S(1)} %bitcast.237) | data formatting | bytes 12582912
  65.0 6.3 %fusion.37 = f32[16384,96]{0,1:T(8,128)S(1)} fusion(f32[96,16384]{1,0:T(8,128)S(1)} %bitcast.231, f32[1,1,96,96]{3,2,1,0:T(8,128)S(1)} %copy-done), kind=kOutput, calls=%fused_computation.106 | convolution fusion | flops 1811939328 | bytes 12619776 | tf_op jit(solution)/shard_map/dot_general | solution.py:107
  77.6 3.2 %collective-permute-start.9 = (f32[2,6,16,256]{3,2,1,0:T(8,128)S(1)}, f32[2,6,16,256]{3,2,1,0:T(8,128)S(1)}, u32[]{:S(2)}, u32[]{:S(2)}) collective-permute-start(f32[2,6,16,256]{3,2,1,0:T(8,128)S(1)} %pad_maximum_fusion.16), channel_id=1, source_target_pairs={{0,4},{1,5},{2,6},{3,7},{4,0},{5,1},{6,2},{7,3},{8,12},{9,13},{10,... | collective-permute-start | bytes 589832 | tf_op jit(solution)/shard_map/ppermute | solution.py:27
  81.0 6.9 %collective-permute-start.7 = (f32[6,2,256]{2,1,0:T(2,128)S(1)}, f32[6,2,256]{2,1,0:T(2,128)S(1)}, u32[]{:S(2)}, u32[]{:S(2)}) collective-permute-start(f32[6,2,256]{2,1,0:T(2,128)S(1)} %get-tuple-element.20), channel_id=1, source_target_pairs={{1,0},{2,1},{3,2},{4,3},{5,4},{6,5},{7,6},{8,7},{9,8},{10,9},{11,1... | collective-permute-start | bytes 36872 | tf_op jit(solution)/shard_map/ppermute | solution.py:19
  95.9 5.1 %fusion.28 = f32[6,16,64,256]{3,2,0,1:T(8,128)S(1)} fusion(f32[6,1,64,256]{3,2,0,1:T(8,128)S(1)} %get-tuple-element.8, f32[6,16,64,256]{3,2,0,1:T(8,128)} %copy-done.1, f32[6,1,64,256]{3,2,0,1:T(8,128)S(1)} %get-tuple-element.7), kind=kLoop, calls=%fused_computation.53 | loop fusion | flops 4718592 | bytes 13369344 | tf_op jit(solution)/shard_map/sub | solution.py:56
  101.0 12.6 %fusion.2 = f32[16,64,256,6]{2,3,1,0:T(8,128)} fusion(f32[6,16,64,256]{3,2,0,1:T(8,128)S(1)} %fusion.28, f32[1,1,6,6]{3,1,2,0:T(1,128)S(1)} %copy-done.10), kind=kOutput, calls=%fused_computation.8 | convolution fusion | flops 113246208 | bytes 12583056 | tf_op jit(solution)/shard_map/vw,wijk->vijk/dot_general | solution.py:57
  113.6 12.1 %fusion.15 = f32[6,16,64,256]{3,2,0,1:T(8,128)S(1)} fusion(f32[6,16,64,256]{3,2,0,1:T(8,128)S(1)} %bitcast.209, f32[6,16,1,256]{3,2,0,1:T(1,128)} %copy.423, f32[6,16,1,256]{3,2,0,1:T(1,128)} %copy.422, f32[16,64,256,6]{2,3,1,0:T(8,128)} %fusion.2, f32[1,1,6,16,64,256]{5,4,3,2,1,0:T(8,128)S(1)} %bitcast.222, f32[6,1,64,256]{3,2,0,1:T(8,128)} %copy-done.8, ...), kind=kLoop, calls=%fused_computation.21 | loop fusion | flops 22020096 | bytes 27197440 | tf_op jit(solution)/shard_map/sub | solution.py:58
  126.2 4.4 %copy.440 = f32[12,8,64,256]{3,1,2,0:T(8,128)S(1)} copy(f32[12,8,64,256]{3,2,1,0:T(8,128)S(1)} %bitcast.238) | data formatting | bytes 12582912
  130.6 6.3 %fusion.35 = f32[16384,96]{0,1:T(8,128)S(1)} fusion(f32[96,16384]{1,0:T(8,128)S(1)} %bitcast.233, f32[1,1,96,96]{3,2,1,0:T(8,128)S(1)} %copy-done), kind=kOutput, calls=%fused_computation.104 | convolution fusion | flops 1811939328 | bytes 12619776 | tf_op jit(solution)/shard_map/dot_general | solution.py:107
  143.4 3.5 %collective-permute-start.15 = (f32[2,6,16,256]{3,2,1,0:T(8,128)S(1)}, f32[2,6,16,256]{3,2,1,0:T(8,128)S(1)}, u32[]{:S(2)}, u32[]{:S(2)}) collective-permute-start(f32[2,6,16,256]{3,2,1,0:T(8,128)S(1)} %pad_maximum_fusion.17), channel_id=1, source_target_pairs={{0,4},{1,5},{2,6},{3,7},{4,0},{5,1},{6,2},{7,3},{8,12},{9,13},{10,... | collective-permute-start | bytes 589832 | tf_op jit(solution)/shard_map/ppermute | solution.py:27
  147.0 6.9 %collective-permute-start.13 = (f32[6,2,256]{2,1,0:T(2,128)S(1)}, f32[6,2,256]{2,1,0:T(2,128)S(1)}, u32[]{:S(2)}, u32[]{:S(2)}) collective-permute-start(f32[6,2,256]{2,1,0:T(2,128)S(1)} %get-tuple-element.18), channel_id=1, source_target_pairs={{1,0},{2,1},{3,2},{4,3},{5,4},{6,5},{7,6},{8,7},{9,8},{10,9},{11,1... | collective-permute-start | bytes 36872 | tf_op jit(solution)/shard_map/ppermute | solution.py:19
  162.0 5.1 %fusion.29 = f32[6,16,64,256]{3,2,0,1:T(8,128)S(1)} fusion(f32[6,1,64,256]{3,2,0,1:T(8,128)S(1)} %get-tuple-element.6, f32[6,16,64,256]{3,2,0,1:T(8,128)} %copy-done.3, f32[6,1,64,256]{3,2,0,1:T(8,128)S(1)} %get-tuple-element.5), kind=kLoop, calls=%fused_computation.54 | loop fusion | flops 4718592 | bytes 13369344 | tf_op jit(solution)/shard_map/sub | solution.py:56
  167.2 12.6 %fusion = f32[16,64,256,6]{2,3,1,0:T(8,128)} fusion(f32[6,16,64,256]{3,2,0,1:T(8,128)S(1)} %fusion.29, f32[1,1,6,6]{3,1,2,0:T(1,128)S(1)} %copy-done.10), kind=kOutput, calls=%fused_computation.6 | convolution fusion | flops 113246208 | bytes 12583056 | tf_op jit(solution)/shard_map/vw,wijk->vijk/dot_general | solution.py:57
  179.8 12.0 %fusion.20 = f32[6,16,64,256]{3,2,0,1:T(8,128)S(1)} fusion(f32[6,16,64,256]{3,2,0,1:T(8,128)S(1)} %bitcast.218, f32[6,16,1,256]{3,2,0,1:T(1,128)} %copy.431, f32[6,16,1,256]{3,2,0,1:T(1,128)S(1)} %copy-done.9, f32[16,64,256,6]{2,3,1,0:T(8,128)} %fusion, f32[1,1,6,16,64,256]{5,4,3,2,1,0:T(8,128)S(1)} %bitcast.224, f32[6,1,64,256]{3,2,0,1:T(8,128)} %copy-done.6, ...), kind=kLoop, calls=%fused_computation.26 | loop fusion | flops 22020096 | bytes 27197440 | tf_op jit(solution)/shard_map/sub | solution.py:58
  192.3 4.4 %copy.443 = f32[12,8,64,256]{3,1,2,0:T(8,128)S(1)} copy(f32[12,8,64,256]{3,2,1,0:T(8,128)S(1)} %bitcast.239) | data formatting | bytes 12582912
  196.7 6.3 %fusion.33 = f32[16384,96]{0,1:T(8,128)S(1)} fusion(f32[96,16384]{1,0:T(8,128)S(1)} %bitcast.235, f32[1,1,96,96]{3,2,1,0:T(8,128)S(1)} %copy-done), kind=kOutput, calls=%fused_computation.102 | convolution fusion | flops 1811939328 | bytes 12619776 | tf_op jit(solution)/shard_map/dot_general | solution.py:107
  203.0 4.8 %copy.444 = f32[12,8,64,256]{3,2,1,0:T(8,128)} copy(f32[12,8,64,256]{3,1,2,0:T(8,128)S(1)} %bitcast.236) | data formatting | bytes 12582912
  207.8 14.5 %add_add_fusion = f32[1,1,6,16,64,256]{5,4,3,2,1,0:T(8,128)} fusion(f32[1,1,6,16,64,256]{5,4,3,2,1,0:T(8,128)} %bitcast.240, f32[1,1,6,16,64,256]{5,4,3,2,1,0:T(8,128)} %bitcast.230, f32[1,1,6,16,64,256]{5,4,3,2,1,0:T(8,128)} %param.9, f32[1,1,6,16,64,256]{5,4,3,2,1,0:T(8,128)} %bitcast.228), kind=kLoop, calls=%fused_computation.51 | loop fusion | flops 4718592 | bytes 31457280 | tf_op jit(solution)/shard_map/add | solution.py:108
  (155 shorter events, 45.7 us)
Async XLA Ops:
  0.0 65.0 %copy-start = (f32[1,1,96,96]{3,2,1,0:T(8,128)S(1)}, f32[1,1,96,96]{3,2,1,0:T(8,128)}, u32[]{:S(2)}) copy-start(f32[1,1,96,96]{3,2,1,0:T(8,128)} %param.13) | copy-start | bytes 110596
  0.0 21.1 %copy-start.11 = (f32[1,1,64,4]{2,3,1,0:T(4,128)S(1)}, f32[1,1,64,4]{2,3,1,0:T(4,128)}, u32[]{:S(2)}) copy-start(f32[1,1,64,4]{2,3,1,0:T(4,128)} %param.15) | copy-start | bytes 3076
  0.0 21.1 %copy-start.12 = (s32[1,1,64,4]{2,3,1,0:T(4,128)S(1)}, s32[1,1,64,4]{2,3,1,0:T(4,128)}, u32[]{:S(2)}) copy-start(s32[1,1,64,4]{2,3,1,0:T(4,128)} %param.14) | copy-start | bytes 3076
  6.4 19.2 %collective-permute-start.5 = (f32[2,6,16,256]{3,2,1,0:T(8,128)S(1)}, f32[2,6,16,256]{3,2,1,0:T(8,128)S(1)}, u32[]{:S(2)}, u32[]{:S(2)}) collective-permute-start(f32[2,6,16,256]{3,2,1,0:T(8,128)S(1)} %pad_maximum_fusion.15), channel_id=1, source_target_pairs={{0,1},{1,0},{2,3},{3,2},{4,5},{5,4},{6,7},{7,6},{8,9},{9,8},{10,11... | collective-permute-start | bytes 589832 | tf_op jit(solution)/shard_map/ppermute | solution.py:27
  8.7 17.0 %collective-permute-start.4 = (f32[2,6,16,256]{3,2,1,0:T(8,128)S(1)}, f32[2,6,16,256]{3,2,1,0:T(8,128)S(1)}, u32[]{:S(2)}, u32[]{:S(2)}) collective-permute-start(f32[2,6,16,256]{3,2,1,0:T(8,128)S(1)} %pad_maximum_fusion.15), channel_id=1, source_target_pairs={{0,2},{1,3},{2,0},{3,1},{4,6},{5,7},{6,4},{7,5},{8,10},{9,11},{10,... | collective-permute-start | bytes 589832 | tf_op jit(solution)/shard_map/ppermute | solution.py:27
  11.3 14.3 %collective-permute-start.3 = (f32[2,6,16,256]{3,2,1,0:T(8,128)S(1)}, f32[2,6,16,256]{3,2,1,0:T(8,128)S(1)}, u32[]{:S(2)}, u32[]{:S(2)}) collective-permute-start(f32[2,6,16,256]{3,2,1,0:T(8,128)S(1)} %pad_maximum_fusion.15), channel_id=1, source_target_pairs={{0,4},{1,5},{2,6},{3,7},{4,0},{5,1},{6,2},{7,3},{8,12},{9,13},{10,... | collective-permute-start | bytes 589832 | tf_op jit(solution)/shard_map/ppermute | solution.py:27
  14.1 8.4 %collective-permute-start = (f32[6,2,256]{2,1,0:T(2,128)S(1)}, f32[6,2,256]{2,1,0:T(2,128)S(1)}, u32[]{:S(2)}, u32[]{:S(2)}) collective-permute-start(f32[6,2,256]{2,1,0:T(2,128)S(1)} %get-tuple-element.21), channel_id=1, source_target_pairs={{0,1},{1,2},{2,3},{3,4},{4,5},{5,6},{6,7},{7,8},{8,9},{9,10},{10,1... | collective-permute-start | bytes 36872 | tf_op jit(solution)/shard_map/ppermute | solution.py:17
  14.2 8.4 %collective-permute-start.1 = (f32[6,2,256]{2,1,0:T(2,128)S(1)}, f32[6,2,256]{2,1,0:T(2,128)S(1)}, u32[]{:S(2)}, u32[]{:S(2)}) collective-permute-start(f32[6,2,256]{2,1,0:T(2,128)S(1)} %get-tuple-element.22), channel_id=1, source_target_pairs={{1,0},{2,1},{3,2},{4,3},{5,4},{6,5},{7,6},{8,7},{9,8},{10,9},{11,1... | collective-permute-start | bytes 36872 | tf_op jit(solution)/shard_map/ppermute | solution.py:19
  22.6 5.2 %collective-permute-start.2 = (f32[6,68,256]{2,1,0:T(8,128)S(1)}, f32[6,68,256]{2,1,0:T(8,128)S(1)}, u32[]{:S(2)}, u32[]{:S(2)}) collective-permute-start(f32[6,68,256]{2,1,0:T(8,128)S(1)} %pad_maximum_fusion.12), channel_id=1, source_target_pairs={{0,64},{64,0},{1,65},{65,1},{2,66},{66,2},{3,67},{67,3},{4,68},{68... | collective-permute-start | bytes 1253384 | tf_op jit(solution)/shard_map/ppermute | solution.py:27
  30.2 17.8 %slice-start.2 = ((s8[6291456]{0:T(1024)(128)(4,1)}), s8[4194304]{0:T(1024)(128)(4,1)S(1)}, s32[]{:S(2)}) async-start(s8[6291456]{0:T(1024)(128)(4,1)} %bitcast.214), calls=%async_computation.2 | async-start | bytes 8388608
  30.2 17.8 %slice-start.6 = ((s8[6291456]{0:T(1024)(128)(4,1)}), s8[4194304]{0:T(1024)(128)(4,1)S(1)}, s32[]{:S(2)}) async-start(s8[6291456]{0:T(1024)(128)(4,1)} %bitcast.219), calls=%async_computation.6 | async-start | bytes 8388608
  77.3 13.9 %collective-permute-start.11 = (f32[2,6,16,256]{3,2,1,0:T(8,128)S(1)}, f32[2,6,16,256]{3,2,1,0:T(8,128)S(1)}, u32[]{:S(2)}, u32[]{:S(2)}) collective-permute-start(f32[2,6,16,256]{3,2,1,0:T(8,128)S(1)} %pad_maximum_fusion.16), channel_id=1, source_target_pairs={{0,1},{1,0},{2,3},{3,2},{4,5},{5,4},{6,7},{7,6},{8,9},{9,8},{10,11... | collective-permute-start | bytes 589832 | tf_op jit(solution)/shard_map/ppermute | solution.py:27
  77.4 13.8 %collective-permute-start.10 = (f32[2,6,16,256]{3,2,1,0:T(8,128)S(1)}, f32[2,6,16,256]{3,2,1,0:T(8,128)S(1)}, u32[]{:S(2)}, u32[]{:S(2)}) collective-permute-start(f32[2,6,16,256]{3,2,1,0:T(8,128)S(1)} %pad_maximum_fusion.16), channel_id=1, source_target_pairs={{0,2},{1,3},{2,0},{3,1},{4,6},{5,7},{6,4},{7,5},{8,10},{9,11},{10,... | collective-permute-start | bytes 589832 | tf_op jit(solution)/shard_map/ppermute | solution.py:27
  77.6 13.6 %collective-permute-start.9 = (f32[2,6,16,256]{3,2,1,0:T(8,128)S(1)}, f32[2,6,16,256]{3,2,1,0:T(8,128)S(1)}, u32[]{:S(2)}, u32[]{:S(2)}) collective-permute-start(f32[2,6,16,256]{3,2,1,0:T(8,128)S(1)} %pad_maximum_fusion.16), channel_id=1, source_target_pairs={{0,4},{1,5},{2,6},{3,7},{4,0},{5,1},{6,2},{7,3},{8,12},{9,13},{10,... | collective-permute-start | bytes 589832 | tf_op jit(solution)/shard_map/ppermute | solution.py:27
  80.9 8.2 %collective-permute-start.6 = (f32[6,2,256]{2,1,0:T(2,128)S(1)}, f32[6,2,256]{2,1,0:T(2,128)S(1)}, u32[]{:S(2)}, u32[]{:S(2)}) collective-permute-start(f32[6,2,256]{2,1,0:T(2,128)S(1)} %get-tuple-element.19), channel_id=1, source_target_pairs={{0,1},{1,2},{2,3},{3,4},{4,5},{5,6},{6,7},{7,8},{8,9},{9,10},{10,1... | collective-permute-start | bytes 36872 | tf_op jit(solution)/shard_map/ppermute | solution.py:17
  81.0 8.1 %collective-permute-start.7 = (f32[6,2,256]{2,1,0:T(2,128)S(1)}, f32[6,2,256]{2,1,0:T(2,128)S(1)}, u32[]{:S(2)}, u32[]{:S(2)}) collective-permute-start(f32[6,2,256]{2,1,0:T(2,128)S(1)} %get-tuple-element.20), channel_id=1, source_target_pairs={{1,0},{2,1},{3,2},{4,3},{5,4},{6,5},{7,6},{8,7},{9,8},{10,9},{11,1... | collective-permute-start | bytes 36872 | tf_op jit(solution)/shard_map/ppermute | solution.py:19
  89.1 4.4 %collective-permute-start.8 = (f32[6,68,256]{2,1,0:T(8,128)S(1)}, f32[6,68,256]{2,1,0:T(8,128)S(1)}, u32[]{:S(2)}, u32[]{:S(2)}) collective-permute-start(f32[6,68,256]{2,1,0:T(8,128)S(1)} %pad_maximum_fusion.13), channel_id=1, source_target_pairs={{0,64},{64,0},{1,65},{65,1},{2,66},{66,2},{3,67},{67,3},{4,68},{68... | collective-permute-start | bytes 1253384 | tf_op jit(solution)/shard_map/ppermute | solution.py:27
  142.9 14.5 %collective-permute-start.17 = (f32[2,6,16,256]{3,2,1,0:T(8,128)S(1)}, f32[2,6,16,256]{3,2,1,0:T(8,128)S(1)}, u32[]{:S(2)}, u32[]{:S(2)}) collective-permute-start(f32[2,6,16,256]{3,2,1,0:T(8,128)S(1)} %pad_maximum_fusion.17), channel_id=1, source_target_pairs={{0,1},{1,0},{2,3},{3,2},{4,5},{5,4},{6,7},{7,6},{8,9},{9,8},{10,11... | collective-permute-start | bytes 589832 | tf_op jit(solution)/shard_map/ppermute | solution.py:27
  143.0 14.4 %collective-permute-start.16 = (f32[2,6,16,256]{3,2,1,0:T(8,128)S(1)}, f32[2,6,16,256]{3,2,1,0:T(8,128)S(1)}, u32[]{:S(2)}, u32[]{:S(2)}) collective-permute-start(f32[2,6,16,256]{3,2,1,0:T(8,128)S(1)} %pad_maximum_fusion.17), channel_id=1, source_target_pairs={{0,2},{1,3},{2,0},{3,1},{4,6},{5,7},{6,4},{7,5},{8,10},{9,11},{10,... | collective-permute-start | bytes 589832 | tf_op jit(solution)/shard_map/ppermute | solution.py:27
  143.4 14.0 %collective-permute-start.15 = (f32[2,6,16,256]{3,2,1,0:T(8,128)S(1)}, f32[2,6,16,256]{3,2,1,0:T(8,128)S(1)}, u32[]{:S(2)}, u32[]{:S(2)}) collective-permute-start(f32[2,6,16,256]{3,2,1,0:T(8,128)S(1)} %pad_maximum_fusion.17), channel_id=1, source_target_pairs={{0,4},{1,5},{2,6},{3,7},{4,0},{5,1},{6,2},{7,3},{8,12},{9,13},{10,... | collective-permute-start | bytes 589832 | tf_op jit(solution)/shard_map/ppermute | solution.py:27
  147.0 8.2 %collective-permute-start.12 = (f32[6,2,256]{2,1,0:T(2,128)S(1)}, f32[6,2,256]{2,1,0:T(2,128)S(1)}, u32[]{:S(2)}, u32[]{:S(2)}) collective-permute-start(f32[6,2,256]{2,1,0:T(2,128)S(1)} %get-tuple-element.17), channel_id=1, source_target_pairs={{0,1},{1,2},{2,3},{3,4},{4,5},{5,6},{6,7},{7,8},{8,9},{9,10},{10,1... | collective-permute-start | bytes 36872 | tf_op jit(solution)/shard_map/ppermute | solution.py:17
  147.0 8.1 %collective-permute-start.13 = (f32[6,2,256]{2,1,0:T(2,128)S(1)}, f32[6,2,256]{2,1,0:T(2,128)S(1)}, u32[]{:S(2)}, u32[]{:S(2)}) collective-permute-start(f32[6,2,256]{2,1,0:T(2,128)S(1)} %get-tuple-element.18), channel_id=1, source_target_pairs={{1,0},{2,1},{3,2},{4,3},{5,4},{6,5},{7,6},{8,7},{9,8},{10,9},{11,1... | collective-permute-start | bytes 36872 | tf_op jit(solution)/shard_map/ppermute | solution.py:19
  155.2 4.4 %collective-permute-start.14 = (f32[6,68,256]{2,1,0:T(8,128)S(1)}, f32[6,68,256]{2,1,0:T(8,128)S(1)}, u32[]{:S(2)}, u32[]{:S(2)}) collective-permute-start(f32[6,68,256]{2,1,0:T(8,128)S(1)} %pad_maximum_fusion.14), channel_id=1, source_target_pairs={{0,64},{64,0},{1,65},{65,1},{2,66},{66,2},{3,67},{67,3},{4,68},{68... | collective-permute-start | bytes 1253384 | tf_op jit(solution)/shard_map/ppermute | solution.py:27
  162.0 17.8 %slice-start.10 = ((s8[6291456]{0:T(1024)(128)(4,1)}), s8[4194304]{0:T(1024)(128)(4,1)S(1)}, s32[]{:S(2)}) async-start(s8[6291456]{0:T(1024)(128)(4,1)} %bitcast.223), calls=%async_computation.10 | async-start | bytes 8388608
  (21 other events, 188.2 us)
where the time goes:
time: 225 us; the launch traced here: 223 us
  other arithmetic  71.9 us (32%)
  matrix products  61.5 us (27%)
  local copies, waits for them, and re-layouts  42.2 us (19%)
  starting transfers between devices  42.1 us (19%)
  waiting for transfers between devices  2.44 us (1%)
  between operations  2.39 us (1%)
    dot_general x3, matrix products, operate(): jnp.einsum('vw,wijk->vijk', advection, stretch, precision=lax.Precision.H...  37.7 us
    sub x3, other arithmetic, operate(): return forcing - (stiffness[None] * field - neighbours + carried)  36.2 us
    unnamed x61, local copies, waits for them, and re-layouts  34.3 us
    ppermute x12, starting transfers between devices, from_partner(): lax.ppermute(value, axis, [(i, i ^ 1 << stride) for i in range(lax.axis_s...  21.2 us
    ppermute x3, starting transfers between devices, padded(): lax.ppermute(head, axis, [((i + 1) % count, i) for i in range(count)])  20.6 us
    dot_general x3, matrix products, body(): change = jnp.dot(inverse, flat, precision=lax.Precision.HIGHEST)  18.8 us
    add x3, other arithmetic, body(): field = field + change.reshape(field.shape)  18.3 us
    sub x3, other arithmetic, operate(): stretch = along_i[:, 2:] - along_i[:, :-2]  15.4 us
  transfers between devices with their start and end apart: 18, of which 2 were waited for; matrix products, arithmetic and copies ran while one was open for 4% of the time, Pallas kernels for 0%

commit v1 on v0

v1 whole, which is shorter than its diff:
```python
import jax
import jax.numpy as jnp
from jax import lax
from jax.experimental import pallas as pl
from jax.experimental.pallas import tpu as pltpu
from jax.sharding import PartitionSpec as P

SWEEPS = 3
NV, NI, NJ, NK = 6, 16, 64, 256
LN = NV * NI
F32, BF16 = jnp.float32, jnp.bfloat16
VM = pl.BlockSpec(memory_space=pltpu.VMEM)
SM = pl.BlockSpec(memory_space=pltpu.SMEM)
HI = lax.Precision.HIGHEST
BLOCK = 4


def params(mib):
    return pltpu.CompilerParams(vmem_limit_bytes=mib << 20)


def iota(shape, dim):
    return lax.broadcasted_iota(jnp.int32, shape, dim)


def hot(mask):
    return jnp.where(mask, 1.0, 0.0).astype(F32)


def high_part(x):
    return x.astype(BF16).astype(F32)


def dot_exact(a, b):
    return jnp.dot(a, b, precision=HI, preferred_element_type=F32)


def prepare_kernel(flags, inverse, jacobian, sweep_w, ghost_w, face_w, flip_w):
    rotor = flags[0] == 0
    code = flags[1]
    lines = inverse[...]
    r, c = iota((LN, LN), 0), iota((LN, LN), 1)
    rv, ri, cv, ci = r // NI, r % NI, c // NI, c % NI
    expand = hot(iota((LN, 8), 0) // NI == iota((LN, 8), 1))
    collect = hot(iota((8, LN), 1) // NI == iota((8, LN), 0))
    flux = dot_exact(dot_exact(expand, jacobian[...]), collect)
    last = NI - 1
    self_above = jnp.logical_and(ri == last, ci == last)
    self_below = jnp.logical_and(ri == 0, ci == 0)
    is_rotor = jnp.where(rotor, 1.0, 0.0)
    above = hot(ci == ri + 1) + hot(self_above) * (1.0 - is_rotor)
    below = hot(ri == ci + 1) + hot(self_below) * is_rotor
    along = hot(rv == cv) * (above + below) - 0.5 * flux * (above - below)
    both = dot_exact(lines, along)
    sign = jnp.where(rotor, 1.0, -1.0)
    edge = jnp.where(rotor, last, 0)
    g_row, g_col = iota((LN, 8), 0), iota((LN, 8), 1)
    spread = hot(g_row % NI == edge) * (
        hot(jnp.logical_and(g_row // NI == g_col, g_col < NV))
        - 0.5 * sign * dot_exact(expand, jacobian[...])
    )
    ghost = dot_exact(lines, spread)
    turned = dot_exact(lines, hot(jnp.logical_and(rv == cv, ri + ci == last)))
    face = jnp.where(code % 2 == 1, turned, lines)

    def place(rows, cols, starts):
        k, m = iota((rows, cols), 0), iota((rows, cols), 1)
        total = hot(m == k + starts[0])
        for start in starts[1:]:
            total = total + hot(m == k + start)
        return total

    def split(matrix):
        top = high_part(matrix)
        return top, high_part(matrix - top)

    l_hi, l_lo = split(lines)
    b_hi, b_lo = split(both)
    width = 4 * LN
    sweep_w[:LN] = (
        dot_exact(l_hi, place(LN, width, (0, LN)))
        + dot_exact(b_hi, place(LN, width, (2 * LN, 3 * LN)))
    ).astype(BF16)
    sweep_w[LN:] = (
        dot_exact(l_lo, place(LN, width, (0,))) + dot_exact(b_lo, place(LN, width, (2 * LN,)))
    ).astype(BF16)
    g_hi, g_lo = split(ghost)
    ghost_w[:LN] = dot_exact(g_hi, place(8, 16, (0, 8))).astype(BF16)
    ghost_w[LN:] = dot_exact(g_lo, place(8, 16, (0,))).astype(BF16)
    f_hi, f_lo = split(face)
    face_w[:LN] = dot_exact(f_hi, place(LN, 2 * LN, (0, LN))).astype(BF16)
    face_w[LN:] = dot_exact(f_lo, place(LN, 2 * LN, (0,))).astype(BF16)
    a, b = iota((NK, NK), 0), iota((NK, NK), 1)
    mirrored = hot(a + b == NK - 1)
    flip_w[...] = jnp.where(code // 2 == 1, mirrored, hot(a == b)).astype(BF16)


def prepare(flags, inverse, jacobian):
    return pl.pallas_call(
        prepare_kernel,
        out_shape=[
            pltpu.VMEM((2 * LN, 4 * LN), BF16),
            pltpu.VMEM((2 * LN, 16), BF16),
            pltpu.VMEM((2 * LN, 2 * LN), BF16),
            pltpu.VMEM((NK, NK), BF16),
        ],
        in_specs=[SM, VM, VM],
        out_specs=[VM] * 4,
        compiler_params=params(6),
        name="prepare",
    )(flags, inverse, jacobian)


def halves(x):
    top = x.astype(BF16)
    return top, (x - top.astype(F32)).astype(BF16)


def shifted(x):
    half = NK // 2
    a, b = x[:, :half], x[:, half:]
    lane = iota((8, half), 1)
    first = jnp.tile(lane == 0, (x.shape[0] // 8, 1))
    end = jnp.tile(lane == half - 1, (x.shape[0] // 8, 1))
    ra, rb = pltpu.roll(a, 1, 1), pltpu.roll(b, 1, 1)
    la, lb = pltpu.roll(a, half - 1, 1), pltpu.roll(b, half - 1, 1)
    zero = jnp.zeros_like(a)
    left = [jnp.where(first, zero, ra), jnp.where(first, ra, rb)]
    right = [jnp.where(end, lb, la), jnp.where(end, zero, lb)]
    return jnp.concatenate([left[0] + right[0], left[1] + right[1]], axis=1)


def interior_kernel(state, source, diagonal, weights, out, stack):
    def block(step, carry):
        base = step * BLOCK
        for n in range(BLOCK):
            j = base + n
            s = state[j]
            below = state[jnp.maximum(j - 1, 0)]
            above = state[jnp.minimum(j + 1, NJ - 1)]
            if n == 0:
                below = below * jnp.where(j == 0, 0.0, 1.0)
            if n == BLOCK - 1:
                above = above * jnp.where(j == NJ - 1, 0.0, 1.0)
            d = jnp.concatenate([diagonal[j]] * NV, axis=0)
            e = source[j] - d * s + (below + above) + shifted(s)
            e_hi, e_lo = halves(e)
            s_hi, s_lo = halves(s)
            cols = pl.ds(n * NK, NK)
            stack[0:LN, cols] = e_hi
            stack[LN : 2 * LN, cols] = e_lo
            stack[2 * LN : 3 * LN, cols] = s_hi
            stack[3 * LN :, cols] = s_lo
        for n in range(BLOCK):
            cols = pl.ds(n * NK, NK)
            both = jnp.dot(weights[...], stack[:, cols], preferred_element_type=F32)
            out[base + n] = state[base + n] + (both[:LN] + both[LN:])
        return carry

    lax.fori_loop(0, NJ // BLOCK, block, 0)


def interior(state, source, diagonal, weights):
    return pl.pallas_call(
        interior_kernel,
        out_shape=pltpu.VMEM((NJ, LN, NK), F32),
        in_specs=[VM] * 4,
        out_specs=VM,
        scratch_shapes=[pltpu.VMEM((4 * LN, BLOCK * NK), BF16)],
        compiler_params=params(4),
        cost_estimate=pl.CostEstimate(flops=4_800_000_000, bytes_accessed=14_000_000, transcendentals=0),
        name="interior",
    )(state, source, diagonal, weights)


def outer_kernel(coef, edge, part, plane, lo, hi, faces, ghost_w, face_w, flip_w, out, face_out, plane_out, window, stack):
    window[0:2] = lo[...]
    window[2 : NJ + 2] = plane[...]
    window[NJ + 2 :] = hi[...]
    rotor_side = edge[0] == 0

    def pick(x):
        rows = [jnp.where(rotor_side, x[v * NI + NI - 1 : v * NI + NI], x[v * NI : v * NI + 1]) for v in range(NV)]
        return jnp.concatenate(rows + [rows[-1], rows[-1]], axis=0)

    def ghost_of(j):
        total = coef[j, 0] * window[j]
        for d in range(1, 5):
            total = total + coef[j, d] * window[j + d]
        return total

    def block(step, carry):
        base = step * BLOCK
        for n in range(BLOCK):
            g_hi, g_lo = halves(ghost_of(base + n))
            g = jnp.concatenate([g_hi.astype(F32), g_lo.astype(F32)], axis=0).astype(BF16)
            both = jnp.dot(ghost_w[...], g, preferred_element_type=F32)
            out[base + n] = part[base + n] + (both[:LN] + both[LN:])
        return carry

    lax.fori_loop(0, NJ // BLOCK, block, 0)
    for side, j in ((1, 0), (0, NJ - 1)):
        f_hi, f_lo = halves(faces[side])
        stack[:LN] = f_hi
        stack[LN:] = f_lo
        turned = jnp.dot(stack[...], flip_w[...], preferred_element_type=F32).astype(BF16)
        both = jnp.dot(face_w[...], turned, preferred_element_type=F32)
        out[j] = out[j] + (both[:LN] + both[LN:])
    face_out[0] = out[0]
    face_out[1] = out[NJ - 1]

    def planes(step, carry):
        for n in range(BLOCK):
            plane_out[step * BLOCK + n] = pick(out[step * BLOCK + n])
        return carry

    lax.fori_loop(0, NJ // BLOCK, planes, 0)


def outer(coef, edge, part, plane, lo, hi, faces, ghost_w, face_w, flip_w):
    return pl.pallas_call(
        outer_kernel,
        out_shape=[
            pltpu.VMEM((NJ, LN, NK), F32),
            pltpu.VMEM((2, LN, NK), F32),
            pltpu.VMEM((NJ, 8, NK), F32),
        ],
        in_specs=[SM, SM] + [VM] * 8,
        out_specs=[VM] * 3,
        scratch_shapes=[pltpu.VMEM((NJ + 4, 8, NK), F32), pltpu.VMEM((2 * LN, NK), BF16)],
        input_output_aliases={2: 0},
        compiler_params=params(4),
        name="outer",
    )(coef, edge, part, plane, lo, hi, faces, ghost_w, face_w, flip_w)


def exchange(faces, plane, bit, blocks):
    def across(step):
        return [
            (r * blocks + b, (1 - r) * blocks + (b + step) % blocks)
            for r in range(2)
            for b in range(blocks)
        ]

    axes = ("row", "blk")
    lo = lax.ppermute(plane[NJ - 2 :], axes, across(1))
    hi = lax.ppermute(plane[:2], axes, across(-1))
    other = lax.ppermute(plane, "row", [(0, 1), (1, 0)])
    got = [lax.ppermute(faces, "blk", [(b, b ^ (1 << k)) for b in range(blocks)]) for k in range(3)]
    received = jnp.where(bit == 0, got[0], jnp.where(bit == 1, got[1], got[2]))
    return lo, hi, other, received


def body(flow_state, forcing, stiffness, advection, line_inverse, margin_rows, margin_weights, partner_bit, turn_code):
    blocks = lax.axis_size("blk")
    row = lax.axis_index("row")
    field = flow_state[0, 0]
    faces = jnp.stack([field[:, :, 0].reshape(LN, NK), field[:, :, NJ - 1].reshape(LN, NK)])
    plane = jnp.where(row == 0, field[:, NI - 1], field[:, 0])
    plane = jnp.pad(plane.transpose(1, 0, 2), ((0, 0), (0, 2), (0, 0)))
    comm = exchange(faces, plane, partner_bit[0, 0], blocks)
    state = field.reshape(LN, NJ, NK).transpose(1, 0, 2)
    source = forcing[0, 0].reshape(LN, NJ, NK).transpose(1, 0, 2)
    diagonal = stiffness[0, 0].transpose(1, 0, 2)
    slots = margin_rows[0, 0] - jnp.arange(NJ, dtype=jnp.int32)[:, None]
    coef = jnp.sum(
        jnp.where(slots[..., None] == jnp.arange(5, dtype=jnp.int32), margin_weights[0, 0][..., None], 0.0), axis=1
    )
    edge = row.reshape(1)
    flags = jnp.stack([row, turn_code[0, 0]])
    jac = jnp.pad(advection[0, 0], ((0, 2), (0, 2)))
    sweep_w, ghost_w, face_w, flip_w = prepare(flags, line_inverse[0, 0], jac)
    for sweep in range(SWEEPS):
        part = interior(state, source, diagonal, sweep_w)
        lo, hi, other, received = comm
        state, faces, plane = outer(coef, edge, part, other, lo, hi, received, ghost_w, face_w, flip_w)
        if sweep < SWEEPS - 1:
            comm = exchange(faces, plane, partner_bit[0, 0], blocks)
    return state.transpose(1, 0, 2).reshape(field.shape)[None, None]


def solution(mesh):
    return jax.shard_map(
        body,
        mesh=mesh,
        in_specs=(P("row", "blk"),) * 9,
        out_specs=P("row", "blk"),
        check_vma=False,
    )
```

time: 225 us -> 137 us (0.61); the launches traced: 223 us -> 137 us
  other arithmetic: 71.9 us -> 1.5 us
  matrix products: 61.5 us -> 0 us
  Pallas kernels: 0 us -> 48.9 us
  waiting for transfers between devices: 2.44 us -> 25.6 us
  starting transfers between devices: 42.1 us -> 20.3 us
  local copies, waits for them, and re-layouts: 42.2 us -> 39.1 us
    dot_general x9 -> x0, matrix products: 61.5 us -> none  [the longest x3 37.7 us: operate(): jnp.einsum('vw,wijk->vijk', advection, stretch, precision=lax.Precision.H...]
    sub x6 -> x1, other arithmetic: 51.6 us -> 0.01 us  [body(): slots = margin_rows[0, 0] - jnp.arange(NJ, dtype=jnp.int32)[:, None]]
    pallas_call x0 -> x7, Pallas kernels: none -> 48.9 us  [the longest x3 27.1 us: interior(): pl.pallas_call(interior_kernel, out_shape=pltpu.VMEM((NJ, LN, NK), F32),...]
    ppermute x18, waiting for transfers between devices: 2.44 us -> 25.6 us  [the longest x3 23.4 us: exchange(): lo = lax.ppermute(plane[NJ - 2:], axes, across(1))]
    ppermute x18, starting transfers between devices: 42.1 us -> 20.3 us  [the longest x3 10.6 us: exchange(): hi = lax.ppermute(plane[:2], axes, across(-1))]
    add x3 -> x0, other arithmetic: 18.3 us -> none  [body(): field = field + change.reshape(field.shape)]
    another operation x1, local copies, waits for them, and re-layouts: 0.02 us -> 6.28 us  [body(): return state.transpose(1, 0, 2).reshape(field.shape)[None, None]]
    broadcast_in_dim x6 -> x0, local copies, waits for them, and re-layouts: 4.49 us -> none  [the longest x3 2.26 us: operate(): upper_ghost[:, :, None, :]]
  transfers between devices with their start and end apart: 18 -> 18, of which waited for: 2 -> 5; matrix products, arithmetic and copies ran while one was open for 4% -> 9% of each run, Pallas kernels for 0% -> 21%
where the time goes in v1:
time: 137 us
  Pallas kernels  48.9 us (36%)
  local copies, waits for them, and re-layouts  39.1 us (29%)
  waiting for transfers between devices  25.6 us (19%)
  starting transfers between devices  20.3 us (15%)
  between operations  1.7 us (1%)
  other arithmetic  1.5 us (1%)
    unnamed x33, local copies, waits for them, and re-layouts  32.6 us
    pallas_call x3, Pallas kernels, interior(): pl.pallas_call(interior_kernel, out_shape=pltpu.VMEM((NJ, LN, NK), F32),...  27.1 us
    ppermute x3, waiting for transfers between devices, exchange(): lo = lax.ppermute(plane[NJ - 2:], axes, across(1))  23.4 us
    pallas_call x3, Pallas kernels, outer(): pl.pallas_call(outer_kernel, out_shape=[pltpu.VMEM((NJ, LN, NK), F32), pl...  19.8 us
    ppermute x3, starting transfers between devices, exchange(): hi = lax.ppermute(plane[:2], axes, across(-1))  10.6 us
    ppermute x9, starting transfers between devices, exchange(): lax.ppermute(faces, 'blk', [(b, b ^ 1 << k) for b in range(blocks)])  7.12 us
    another operation x1, local copies, waits for them, and re-layouts, body(): return state.transpose(1, 0, 2).reshape(field.shape)[None, None]  6.28 us
  transfers between devices with their start and end apart: 18, of which 5 were waited for; matrix products, arithmetic and copies ran while one was open for 9% of the time, Pallas kernels for 21%

profile of v1, /device:TPU:1, one launch (start us, length us, event | category | flops | bytes accessed | tf_op | source)
XLA Modules:
  0.0 137.1 jit_solution(11930636351797066795)
XLA Ops:
  0.0 7.4 %copy.36 = f32[1,1,6,16,64,256]{5,2,4,3,1,0:T(8,128)S(1)} copy(f32[1,1,6,16,64,256]{5,4,3,2,1,0:T(8,128)} %param.9) | data formatting | bytes 12582912 | tf_op args[0]
  7.4 3.3 %copy-done.7 = f32[1,1,6,16,64,256]{5,2,4,3,1,0:T(8,128)} copy-done((f32[1,1,6,16,64,256]{5,2,4,3,1,0:T(8,128)}, f32[1,1,6,16,64,256]{5,2,4,3,1,0:T(8,128)S(1)}, u32[]{:S(2)}) %copy-start.7) | copy-done | bytes 6291480
  10.8 2.5 %collective-permute-start.5 = (f32[2,96,256]{2,1,0:T(8,128)S(1)}, f32[2,96,256]{2,1,0:T(8,128)S(1)}, u32[]{:S(2)}, u32[]{:S(2)}) collective-permute-start(f32[2,96,256]{2,1,0:T(8,128)S(1)} %pad_maximum_fusion), channel_id=1, source_target_pairs={{0,4},{1,5},{2,6},{3,7},{4,0},{5,1},{6,2},{7,3},{8,12},{9,13},{10,... | collective-permute-start | bytes 589832 | tf_op jit(solution)/shard_map/ppermute | solution.py:249
  13.4 2.9 %collective-permute-start.4 = (f32[2,96,256]{2,1,0:T(8,128)S(1)}, f32[2,96,256]{2,1,0:T(8,128)S(1)}, u32[]{:S(2)}, u32[]{:S(2)}) collective-permute-start(f32[2,96,256]{2,1,0:T(8,128)S(1)} %pad_maximum_fusion), channel_id=1, source_target_pairs={{0,2},{1,3},{2,0},{3,1},{4,6},{5,7},{6,4},{7,5},{8,10},{9,11},{10,... | collective-permute-start | bytes 589832 | tf_op jit(solution)/shard_map/ppermute | solution.py:249
  18.0 5.7 %collective-permute-start.2 = (f32[2,8,256]{2,1,0:T(8,128)S(1)}, f32[2,8,256]{2,1,0:T(8,128)S(1)}, u32[]{:S(2)}, u32[]{:S(2)}) collective-permute-start(f32[2,8,256]{2,1,0:T(8,128)S(1)} %get-tuple-element.33), channel_id=1, source_target_pairs={{0,127},{1,64},{2,65},{3,66},{4,67},{5,68},{6,69},{7,70},{8,71},{9... | collective-permute-start | bytes 49160 | tf_op jit(solution)/shard_map/ppermute | solution.py:247
  24.1 6.6 %copy.22 = f32[1,1,6,16,64,256]{5,3,2,4,1,0:T(8,128)S(1)} copy(f32[1,1,6,16,64,256]{5,4,3,2,1,0:T(8,128)} %param.9) | data formatting | bytes 12582912 | tf_op args[0]
  32.0 3.6 %copy.23 = f32[1,1,6,16,64,256]{5,3,2,4,1,0:T(8,128)S(1)} copy(f32[1,1,6,16,64,256]{5,4,3,2,1,0:T(8,128)S(1)} %bitcast.47) | data formatting | bytes 12582912 | tf_op args[1]
  35.7 1.9 %prepare.1 = (bf16[192,384]{1,0:T(8,128)(2,1)S(1)}, bf16[192,16]{1,0:T(8,128)(2,1)S(1)}, bf16[192,192]{1,0:T(8,128)(2,1)S(1)}, bf16[256,256]{1,0:T(8,128)(2,1)S(1)}) custom-call(s32[2]{0:T(128)S(1)} %pad_add_fusion.flags, f32[96,96]{1,0:T(8,128)S(1)} %bitcast.43, f32[8,8]{1,0:T(8,128)S(1)} %pad.8.jacobian), custom_call_target="tpu_custom_call" | custom-call | tf_op jit(solution)/shard_map/prepare/pallas_call | solution.py:99
  37.7 9.1 %interior.3.part = f32[64,96,256]{2,1,0:T(8,128)S(1)} custom-call(f32[64,96,256]{2,1,0:T(8,128)S(1)} %bitcast.39, f32[64,96,256]{2,1,0:T(8,128)S(1)} %bitcast.35, f32[64,16,256]{2,1,0:T(8,128)S(1)} %bitcast.40, bf16[192,384]{1,0:T(8,128)(2,1)S(1)} %get-tuple-element.16.weights), custom_call_target="tpu_custom_call" | custom-call | flops 4800000000 | bytes 14000000 | tf_op jit(solution)/shard_map/interior/pallas_call | solution.py:164
  46.9 2.7 %copy-done.2 = f32[64,96,256]{2,1,0:T(8,128)} copy-done((f32[64,96,256]{2,1,0:T(8,128)}, f32[64,96,256]{2,1,0:T(8,128)S(1)}, u32[]{:S(2)}) %copy-start.2) | copy-done | bytes 6291480
  50.5 8.8 %collective-permute-done.1.lo = f32[2,8,256]{2,1,0:T(8,128)S(1)} collective-permute-done((f32[2,8,256]{2,1,0:T(8,128)S(1)}, f32[2,8,256]{2,1,0:T(8,128)S(1)}, u32[]{:S(2)}, u32[]{:S(2)}) %collective-permute-start.1) | collective-permute-done | bytes 16416 | tf_op jit(solution)/shard_map/ppermute | solution.py:246
  59.4 2.8 %copy-done.3 = f32[64,96,256]{2,1,0:T(8,128)S(1)} copy-done((f32[64,96,256]{2,1,0:T(8,128)S(1)}, f32[64,96,256]{2,1,0:T(8,128)}, u32[]{:S(2)}) %copy-start.3) | copy-done | bytes 6291480
  62.1 6.3 %outer.3 = (f32[64,96,256]{2,1,0:T(8,128)S(1)}, f32[2,96,256]{2,1,0:T(8,128)S(1)}, f32[64,8,256]{2,1,0:T(8,128)S(1)}) custom-call(f32[64,5]{1,0:T(8,128)S(1)} %copy.30.coef, s32[1]{0:T(128)} %bitcast.2.edge, f32[64,96,256]{2,1,0:T(8,128)S(1)} %copy-done.3, f32[64,8,256]{2,1,0:T(8,128)S(1)} %collective-permute-done.plane, ...), custom_call_target="tpu_custom_call", output_to_operand_aliasing={{0}: (2, {})} | custom-call | tf_op jit(solution)/shard_map/outer/pallas_call | solution.py:221
  68.5 2.7 %copy-done.4 = f32[64,96,256]{2,1,0:T(8,128)} copy-done((f32[64,96,256]{2,1,0:T(8,128)}, f32[64,96,256]{2,1,0:T(8,128)S(1)}, u32[]{:S(2)}) %copy-start.4) | copy-done | bytes 6291480
  72.0 2.8 %copy-done.5 = f32[64,96,256]{2,1,0:T(8,128)S(1)} copy-done((f32[64,96,256]{2,1,0:T(8,128)S(1)}, f32[64,96,256]{2,1,0:T(8,128)}, u32[]{:S(2)}) %copy-start.5) | copy-done | bytes 6291480
  74.8 9.0 %interior.4.part = f32[64,96,256]{2,1,0:T(8,128)S(1)} custom-call(f32[64,96,256]{2,1,0:T(8,128)S(1)} %copy-done.5, f32[64,96,256]{2,1,0:T(8,128)S(1)} %bitcast.36, f32[64,16,256]{2,1,0:T(8,128)S(1)} %bitcast.41, bf16[192,384]{1,0:T(8,128)(2,1)S(1)} %get-tuple-element.16.weights), custom_call_target="tpu_custom_call" | custom-call | flops 4800000000 | bytes 14000000 | tf_op jit(solution)/shard_map/interior/pallas_call | solution.py:164
  85.6 1.4 collective-permute-done.8.hi
  87.0 6.8 %collective-permute-done.7.lo = f32[2,8,256]{2,1,0:T(8,128)S(1)} collective-permute-done((f32[2,8,256]{2,1,0:T(8,128)S(1)}, f32[2,8,256]{2,1,0:T(8,128)S(1)}, u32[]{:S(2)}, u32[]{:S(2)}) %collective-permute-start.7) | collective-permute-done | bytes 16416 | tf_op jit(solution)/shard_map/ppermute | solution.py:246
  93.8 6.3 %outer.4 = (f32[64,96,256]{2,1,0:T(8,128)S(1)}, f32[2,96,256]{2,1,0:T(8,128)S(1)}, f32[64,8,256]{2,1,0:T(8,128)S(1)}) custom-call(f32[64,5]{1,0:T(8,128)S(1)} %copy.30.coef, s32[1]{0:T(128)} %bitcast.2.edge, f32[64,96,256]{2,1,0:T(8,128)S(1)} %interior.4.part, f32[64,8,256]{2,1,0:T(8,128)S(1)} %collective-permute-done.6.plane, ...), custom_call_target="tpu_custom_call", output_to_operand_aliasing={{0}: (2, {})} | custom-call | tf_op jit(solution)/shard_map/outer/pallas_call | solution.py:221
  102.2 9.0 %interior.5.part = f32[64,96,256]{2,1,0:T(8,128)S(1)} custom-call(f32[64,96,256]{2,1,0:T(8,128)S(1)} %get-tuple-element.23.state, f32[64,96,256]{2,1,0:T(8,128)S(1)} %bitcast.37, f32[64,16,256]{2,1,0:T(8,128)S(1)} %bitcast.42, bf16[192,384]{1,0:T(8,128)(2,1)S(1)} %get-tuple-element.16.weights), custom_call_target="tpu_custom_call" | custom-call | flops 4800000000 | bytes 14000000 | tf_op jit(solution)/shard_map/interior/pallas_call | solution.py:164
  111.3 3.6 %collective-permute-start.14 = (f32[2,8,256]{2,1,0:T(8,128)S(1)}, f32[2,8,256]{2,1,0:T(8,128)S(1)}, u32[]{:S(2)}, u32[]{:S(2)}) collective-permute-start(f32[2,8,256]{2,1,0:T(8,128)S(1)} %get-tuple-element.29), channel_id=1, source_target_pairs={{0,127},{1,64},{2,65},{3,66},{4,67},{5,68},{6,69},{7,70},{8,71},{9... | collective-permute-start | bytes 49160 | tf_op jit(solution)/shard_map/ppermute | solution.py:247
  115.8 7.8 %collective-permute-done.13.lo = f32[2,8,256]{2,1,0:T(8,128)S(1)} collective-permute-done((f32[2,8,256]{2,1,0:T(8,128)S(1)}, f32[2,8,256]{2,1,0:T(8,128)S(1)}, u32[]{:S(2)}, u32[]{:S(2)}) %collective-permute-start.13) | collective-permute-done | bytes 16416 | tf_op jit(solution)/shard_map/ppermute | solution.py:246
  123.6 7.2 %outer.5 = (f32[64,96,256]{2,1,0:T(8,128)S(1)}, f32[2,96,256]{2,1,0:T(8,128)}, f32[64,8,256]{2,1,0:T(8,128)}) custom-call(f32[64,5]{1,0:T(8,128)S(1)} %copy.30.coef, s32[1]{0:T(128)} %bitcast.2.edge, f32[64,96,256]{2,1,0:T(8,128)S(1)} %interior.5.part, f32[64,8,256]{2,1,0:T(8,128)S(1)} %collective-permute-done.12.plane, ...), custom_call_target="tpu_custom_call", output_to_operand_aliasing={{0}: (2, {})} | custom-call | tf_op jit(solution)/shard_map/outer/pallas_call | solution.py:221
  130.8 6.3 %copy.31 = f32[1,1,6,16,64,256]{5,4,3,2,1,0:T(8,128)} copy(f32[1,1,6,16,64,256]{5,3,2,4,1,0:T(8,128)S(1)} %bitcast.38) | data formatting | bytes 12582912 | tf_op jit(solution)/shard_map/broadcast_in_dim;reshape | solution.py:279
  (71 shorter events, 8.8 us)
Async XLA Ops:
  10.8 39.5 %collective-permute-start.5 = (f32[2,96,256]{2,1,0:T(8,128)S(1)}, f32[2,96,256]{2,1,0:T(8,128)S(1)}, u32[]{:S(2)}, u32[]{:S(2)}) collective-permute-start(f32[2,96,256]{2,1,0:T(8,128)S(1)} %pad_maximum_fusion), channel_id=1, source_target_pairs={{0,4},{1,5},{2,6},{3,7},{4,0},{5,1},{6,2},{7,3},{8,12},{9,13},{10,... | collective-permute-start | bytes 589832 | tf_op jit(solution)/shard_map/ppermute | solution.py:249
  13.4 37.1 %collective-permute-start.4 = (f32[2,96,256]{2,1,0:T(8,128)S(1)}, f32[2,96,256]{2,1,0:T(8,128)S(1)}, u32[]{:S(2)}, u32[]{:S(2)}) collective-permute-start(f32[2,96,256]{2,1,0:T(8,128)S(1)} %pad_maximum_fusion), channel_id=1, source_target_pairs={{0,2},{1,3},{2,0},{3,1},{4,6},{5,7},{6,4},{7,5},{8,10},{9,11},{10,... | collective-permute-start | bytes 589832 | tf_op jit(solution)/shard_map/ppermute | solution.py:249
  16.3 34.2 %collective-permute-start.3 = (f32[2,96,256]{2,1,0:T(8,128)S(1)}, f32[2,96,256]{2,1,0:T(8,128)S(1)}, u32[]{:S(2)}, u32[]{:S(2)}) collective-permute-start(f32[2,96,256]{2,1,0:T(8,128)S(1)} %pad_maximum_fusion), channel_id=1, source_target_pairs={{0,1},{1,0},{2,3},{3,2},{4,5},{5,4},{6,7},{7,6},{8,9},{9,8},{10,11... | collective-permute-start | bytes 589832 | tf_op jit(solution)/shard_map/ppermute | solution.py:249
  18.0 32.5 %collective-permute-start.2 = (f32[2,8,256]{2,1,0:T(8,128)S(1)}, f32[2,8,256]{2,1,0:T(8,128)S(1)}, u32[]{:S(2)}, u32[]{:S(2)}) collective-permute-start(f32[2,8,256]{2,1,0:T(8,128)S(1)} %get-tuple-element.33), channel_id=1, source_target_pairs={{0,127},{1,64},{2,65},{3,66},{4,67},{5,68},{6,69},{7,70},{8,71},{9... | collective-permute-start | bytes 49160 | tf_op jit(solution)/shard_map/ppermute | solution.py:247
  23.7 8.3 %slice-start = ((s8[6291456]{0:T(1024)(128)(4,1)}), s8[4194304]{0:T(1024)(128)(4,1)S(1)}, s32[]{:S(2)}) async-start(s8[6291456]{0:T(1024)(128)(4,1)} %bitcast.46), calls=%async_computation | async-start | bytes 8388608
  23.8 8.2 %slice-start.1 = ((s8[6291456]{0:T(1024)(128)(4,1)}), s8[2097152]{0:T(1024)(128)(4,1)S(1)}, s32[]{:S(2)}) async-start(s8[6291456]{0:T(1024)(128)(4,1)} %bitcast.46), calls=%async_computation.1 | async-start | bytes 4194304
  23.8 35.6 %collective-permute-start = (f32[64,8,256]{2,1,0:T(8,128)S(1)}, f32[64,8,256]{2,1,0:T(8,128)S(1)}, u32[]{:S(2)}, u32[]{:S(2)}) collective-permute-start(f32[64,8,256]{2,1,0:T(8,128)S(1)} %pad.9), channel_id=1, source_target_pairs={{0,64},{64,0},{1,65},{65,1},{2,66},{66,2},{3,67},{67,3},{4,68},{68... | collective-permute-start | bytes 1572872 | tf_op jit(solution)/shard_map/ppermute | solution.py:248
  35.7 11.2 %copy-start = (f32[1,1,6,16,64,256]{5,3,2,4,1,0:T(8,128)}, f32[1,1,6,16,64,256]{5,3,2,4,1,0:T(8,128)S(1)}, u32[]{:S(2)}) copy-start(f32[1,1,6,16,64,256]{5,3,2,4,1,0:T(8,128)S(1)} %copy.23) | copy-start | bytes 18874372
  37.7 11.9 %copy-start.10 = (s32[1,1,64,4]{2,3,1,0:T(4,128)S(1)}, s32[1,1,64,4]{2,3,1,0:T(4,128)}, u32[]{:S(2)}) copy-start(s32[1,1,64,4]{2,3,1,0:T(4,128)} %param.14) | copy-start | bytes 3076
  37.7 12.5 %copy-start.11 = (f32[1,1,64,4]{2,3,1,0:T(4,128)S(1)}, f32[1,1,64,4]{2,3,1,0:T(4,128)}, u32[]{:S(2)}) copy-start(f32[1,1,64,4]{2,3,1,0:T(4,128)} %param.15) | copy-start | bytes 3076
  50.3 21.7 %copy-start.1 = (f32[1,1,6,16,64,256]{5,3,2,4,1,0:T(8,128)S(1)}, f32[1,1,6,16,64,256]{5,3,2,4,1,0:T(8,128)}, u32[]{:S(2)}) copy-start(f32[1,1,6,16,64,256]{5,3,2,4,1,0:T(8,128)} %copy-done) | copy-start | bytes 18874372
  50.4 9.0 %collective-permute-start.1 = (f32[2,8,256]{2,1,0:T(8,128)S(1)}, f32[2,8,256]{2,1,0:T(8,128)S(1)}, u32[]{:S(2)}, u32[]{:S(2)}) collective-permute-start(f32[2,8,256]{2,1,0:T(8,128)S(1)} %get-tuple-element.34), channel_id=1, source_target_pairs={{0,65},{1,66},{2,67},{3,68},{4,69},{5,70},{6,71},{7,72},{8,73},{9,... | collective-permute-start | bytes 49160 | tf_op jit(solution)/shard_map/ppermute | solution.py:246
  71.2 13.9 %collective-permute-start.11 = (f32[2,96,256]{2,1,0:T(8,128)S(1)}, f32[2,96,256]{2,1,0:T(8,128)S(1)}, u32[]{:S(2)}, u32[]{:S(2)}) collective-permute-start(f32[2,96,256]{2,1,0:T(8,128)S(1)} %get-tuple-element.22), channel_id=1, source_target_pairs={{0,4},{1,5},{2,6},{3,7},{4,0},{5,1},{6,2},{7,3},{8,12},{9,13},{10,... | collective-permute-start | bytes 589832 | tf_op jit(solution)/shard_map/ppermute | solution.py:249
  71.2 14.4 %collective-permute-start.10 = (f32[2,96,256]{2,1,0:T(8,128)S(1)}, f32[2,96,256]{2,1,0:T(8,128)S(1)}, u32[]{:S(2)}, u32[]{:S(2)}) collective-permute-start(f32[2,96,256]{2,1,0:T(8,128)S(1)} %get-tuple-element.22), channel_id=1, source_target_pairs={{0,2},{1,3},{2,0},{3,1},{4,6},{5,7},{6,4},{7,5},{8,10},{9,11},{10,... | collective-permute-start | bytes 589832 | tf_op jit(solution)/shard_map/ppermute | solution.py:249
  71.2 14.4 %collective-permute-start.9 = (f32[2,96,256]{2,1,0:T(8,128)S(1)}, f32[2,96,256]{2,1,0:T(8,128)S(1)}, u32[]{:S(2)}, u32[]{:S(2)}) collective-permute-start(f32[2,96,256]{2,1,0:T(8,128)S(1)} %get-tuple-element.22), channel_id=1, source_target_pairs={{0,1},{1,0},{2,3},{3,2},{4,5},{5,4},{6,7},{7,6},{8,9},{9,8},{10,11... | collective-permute-start | bytes 589832 | tf_op jit(solution)/shard_map/ppermute | solution.py:249
  71.2 22.6 %collective-permute-start.6 = (f32[64,8,256]{2,1,0:T(8,128)S(1)}, f32[64,8,256]{2,1,0:T(8,128)S(1)}, u32[]{:S(2)}, u32[]{:S(2)}) collective-permute-start(f32[64,8,256]{2,1,0:T(8,128)S(1)} %get-tuple-element.21), channel_id=1, source_target_pairs={{0,64},{64,0},{1,65},{65,1},{2,66},{66,2},{3,67},{67,3},{4,68},{68... | collective-permute-start | bytes 1572872 | tf_op jit(solution)/shard_map/ppermute | solution.py:248
  83.8 3.2 %collective-permute-start.8 = (f32[2,8,256]{2,1,0:T(8,128)S(1)}, f32[2,8,256]{2,1,0:T(8,128)S(1)}, u32[]{:S(2)}, u32[]{:S(2)}) collective-permute-start(f32[2,8,256]{2,1,0:T(8,128)S(1)} %get-tuple-element.31), channel_id=1, source_target_pairs={{0,127},{1,64},{2,65},{3,66},{4,67},{5,68},{6,69},{7,70},{8,71},{9... | collective-permute-start | bytes 49160 | tf_op jit(solution)/shard_map/ppermute | solution.py:247
  85.1 8.7 %collective-permute-start.7 = (f32[2,8,256]{2,1,0:T(8,128)S(1)}, f32[2,8,256]{2,1,0:T(8,128)S(1)}, u32[]{:S(2)}, u32[]{:S(2)}) collective-permute-start(f32[2,8,256]{2,1,0:T(8,128)S(1)} %get-tuple-element.32), channel_id=1, source_target_pairs={{0,65},{1,66},{2,67},{3,68},{4,69},{5,70},{6,71},{7,72},{8,73},{9,... | collective-permute-start | bytes 49160 | tf_op jit(solution)/shard_map/ppermute | solution.py:246
  100.1 14.8 %collective-permute-start.17 = (f32[2,96,256]{2,1,0:T(8,128)S(1)}, f32[2,96,256]{2,1,0:T(8,128)S(1)}, u32[]{:S(2)}, u32[]{:S(2)}) collective-permute-start(f32[2,96,256]{2,1,0:T(8,128)S(1)} %get-tuple-element.25), channel_id=1, source_target_pairs={{0,4},{1,5},{2,6},{3,7},{4,0},{5,1},{6,2},{7,3},{8,12},{9,13},{10,... | collective-permute-start | bytes 589832 | tf_op jit(solution)/shard_map/ppermute | solution.py:249
  100.2 14.7 %collective-permute-start.16 = (f32[2,96,256]{2,1,0:T(8,128)S(1)}, f32[2,96,256]{2,1,0:T(8,128)S(1)}, u32[]{:S(2)}, u32[]{:S(2)}) collective-permute-start(f32[2,96,256]{2,1,0:T(8,128)S(1)} %get-tuple-element.25), channel_id=1, source_target_pairs={{0,2},{1,3},{2,0},{3,1},{4,6},{5,7},{6,4},{7,5},{8,10},{9,11},{10,... | collective-permute-start | bytes 589832 | tf_op jit(solution)/shard_map/ppermute | solution.py:249
  100.3 14.6 %collective-permute-start.15 = (f32[2,96,256]{2,1,0:T(8,128)S(1)}, f32[2,96,256]{2,1,0:T(8,128)S(1)}, u32[]{:S(2)}, u32[]{:S(2)}) collective-permute-start(f32[2,96,256]{2,1,0:T(8,128)S(1)} %get-tuple-element.25), channel_id=1, source_target_pairs={{0,1},{1,0},{2,3},{3,2},{4,5},{5,4},{6,7},{7,6},{8,9},{9,8},{10,11... | collective-permute-start | bytes 589832 | tf_op jit(solution)/shard_map/ppermute | solution.py:249
  101.4 22.3 %collective-permute-start.12 = (f32[64,8,256]{2,1,0:T(8,128)S(1)}, f32[64,8,256]{2,1,0:T(8,128)S(1)}, u32[]{:S(2)}, u32[]{:S(2)}) collective-permute-start(f32[64,8,256]{2,1,0:T(8,128)S(1)} %get-tuple-element.24), channel_id=1, source_target_pairs={{0,64},{64,0},{1,65},{65,1},{2,66},{66,2},{3,67},{67,3},{4,68},{68... | collective-permute-start | bytes 1572872 | tf_op jit(solution)/shard_map/ppermute | solution.py:248
  111.3 4.5 %collective-permute-start.14 = (f32[2,8,256]{2,1,0:T(8,128)S(1)}, f32[2,8,256]{2,1,0:T(8,128)S(1)}, u32[]{:S(2)}, u32[]{:S(2)}) collective-permute-start(f32[2,8,256]{2,1,0:T(8,128)S(1)} %get-tuple-element.29), channel_id=1, source_target_pairs={{0,127},{1,64},{2,65},{3,66},{4,67},{5,68},{6,69},{7,70},{8,71},{9... | collective-permute-start | bytes 49160 | tf_op jit(solution)/shard_map/ppermute | solution.py:247
  114.9 8.7 %collective-permute-start.13 = (f32[2,8,256]{2,1,0:T(8,128)S(1)}, f32[2,8,256]{2,1,0:T(8,128)S(1)}, u32[]{:S(2)}, u32[]{:S(2)}) collective-permute-start(f32[2,8,256]{2,1,0:T(8,128)S(1)} %get-tuple-element.30), channel_id=1, source_target_pairs={{0,65},{1,66},{2,67},{3,68},{4,69},{5,70},{6,71},{7,72},{8,73},{9,... | collective-permute-start | bytes 49160 | tf_op jit(solution)/shard_map/ppermute | solution.py:246
  (8 other events, 33.2 us)

commit v2 on v1

v2 whole, which is shorter than its diff:
```python
import functools

import jax
import jax.numpy as jnp
from jax import lax
from jax.experimental import pallas as pl
from jax.experimental.pallas import tpu as pltpu
from jax.sharding import PartitionSpec as P

SWEEPS = 3
NV, NI, NJ, NK = 6, 16, 64, 256
LN = NV * NI
F32, BF16 = jnp.float32, jnp.bfloat16
VM = pl.BlockSpec(memory_space=pltpu.VMEM)
SM = pl.BlockSpec(memory_space=pltpu.SMEM)
ANY = pl.BlockSpec(memory_space=pltpu.HBM)
HI = lax.Precision.HIGHEST
BLOCK = 8
STEPS = NJ // BLOCK


def params(mib):
    return pltpu.CompilerParams(vmem_limit_bytes=mib << 20)


def in_hbm(x):
    return pltpu.with_memory_space_constraint(x, pltpu.HBM)


def iota(shape, dim):
    return lax.broadcasted_iota(jnp.int32, shape, dim)


def hot(mask):
    return jnp.where(mask, 1.0, 0.0).astype(F32)


def high_part(x):
    return x.astype(BF16).astype(F32)


def dot_exact(a, b):
    return jnp.dot(a, b, precision=HI, preferred_element_type=F32)


def mul(a, b):
    return jnp.dot(a, b, preferred_element_type=F32)


def prepare_kernel(flags, inverse, jacobian, sweep_w, ghost_w, edge_w, face_w, flip_w):
    rotor = flags[0] == 0
    code = flags[1]
    lines = inverse[...]
    r, c = iota((LN, LN), 0), iota((LN, LN), 1)
    rv, ri, cv, ci = r // NI, r % NI, c // NI, c % NI
    expand = hot(iota((LN, 8), 0) // NI == iota((LN, 8), 1))
    collect = hot(iota((8, LN), 1) // NI == iota((8, LN), 0))
    flux = dot_exact(dot_exact(expand, jacobian[...]), collect)
    last = NI - 1
    self_above = jnp.logical_and(ri == last, ci == last)
    self_below = jnp.logical_and(ri == 0, ci == 0)
    is_rotor = jnp.where(rotor, 1.0, 0.0)
    above = hot(ci == ri + 1) + hot(self_above) * (1.0 - is_rotor)
    below = hot(ri == ci + 1) + hot(self_below) * is_rotor
    along = hot(rv == cv) * (above + below) - 0.5 * flux * (above - below)
    both = dot_exact(lines, along)
    sign = jnp.where(rotor, 1.0, -1.0)
    edge = jnp.where(rotor, last, 0)
    g_row, g_col = iota((LN, 8), 0), iota((LN, 8), 1)
    spread = hot(g_row % NI == edge) * (
        hot(jnp.logical_and(g_row // NI == g_col, g_col < NV))
        - 0.5 * sign * dot_exact(expand, jacobian[...])
    )
    ghost = dot_exact(lines, spread)
    turned = dot_exact(lines, hot(jnp.logical_and(rv == cv, ri + ci == last)))
    face = jnp.where(code % 2 == 1, turned, lines)

    def place(rows, cols, starts):
        k, m = iota((rows, cols), 0), iota((rows, cols), 1)
        total = hot(m == k + starts[0])
        for start in starts[1:]:
            total = total + hot(m == k + start)
        return total

    def split(matrix):
        top = high_part(matrix)
        return top, high_part(matrix - top)

    l_hi, l_lo = split(lines)
    b_hi, b_lo = split(both)
    width = 4 * LN
    sweep_w[:LN] = (
        dot_exact(l_hi, place(LN, width, (0, LN)))
        + dot_exact(b_hi, place(LN, width, (2 * LN, 3 * LN)))
    ).astype(BF16)
    sweep_w[LN:] = (
        dot_exact(l_lo, place(LN, width, (0,))) + dot_exact(b_lo, place(LN, width, (2 * LN,)))
    ).astype(BF16)
    g_hi, g_lo = split(ghost)
    full = dot_exact(g_hi, place(8, 32, (0, 8))) + dot_exact(g_lo, place(8, 32, (16,)))
    ghost_w[...] = full.astype(BF16)
    pick = hot(jnp.logical_and(iota((16, LN), 1) == NI * iota((16, LN), 0) + edge, iota((16, LN), 0) < NV))
    edge_w[...] = dot_exact(pick, full).astype(BF16)
    f_hi, f_lo = split(face)
    face_w[:LN] = dot_exact(f_hi, place(LN, 2 * LN, (0, LN))).astype(BF16)
    face_w[LN:] = dot_exact(f_lo, place(LN, 2 * LN, (0,))).astype(BF16)
    a, b = iota((NK, NK), 0), iota((NK, NK), 1)
    mirrored = hot(a + b == NK - 1)
    flip_w[...] = jnp.where(code // 2 == 1, mirrored, hot(a == b)).astype(BF16)


def prepare(flags, inverse, jacobian):
    return pl.pallas_call(
        prepare_kernel,
        out_shape=[
            pltpu.VMEM((2 * LN, 4 * LN), BF16),
            pltpu.VMEM((LN, 32), BF16),
            pltpu.VMEM((16, 32), BF16),
            pltpu.VMEM((2 * LN, 2 * LN), BF16),
            pltpu.VMEM((NK, NK), BF16),
        ],
        in_specs=[SM, VM, VM],
        out_specs=[VM] * 5,
        compiler_params=params(6),
        name="prepare",
    )(flags, inverse, jacobian)


HALF = NK // 2


def lanes(h):
    return pl.ds(h * HALF, HALF)


def begin_kernel(edge, state, face_out, plane_out, ends, cut, sems):
    at = edge[0]
    copies = []
    for h in range(2):
        copies.append(pltpu.make_async_copy(state.at[:, 0:8, lanes(h)], ends.at[0, h], sems.at[0, h]))
        copies.append(pltpu.make_async_copy(state.at[:, NJ - 8 : NJ, lanes(h)], ends.at[1, h], sems.at[1, h]))
        for v in range(NV):
            copies.append(pltpu.make_async_copy(state.at[v * NI + at, :, lanes(h)], cut.at[h, v], sems.at[2 + v, h]))
    for copy in copies:
        copy.start()
    for copy in copies:
        copy.wait()
    pad = jnp.zeros((2, HALF), F32)
    for h in range(2):
        for side in range(2):
            rows = ends.at[side, h].reshape(LN * 8, HALF)
            face_out[side, :, lanes(h)] = rows[pl.ds(7 * side, LN, stride=8), :]
        planes = cut.at[h].reshape(NV * NJ, HALF)
        for j in range(NJ):
            plane_out[j, :, lanes(h)] = jnp.concatenate([planes[pl.ds(j, NV, stride=NJ), :], pad], axis=0)


def begin(edge, state):
    return pl.pallas_call(
        begin_kernel,
        out_shape=[pltpu.VMEM((2, LN, NK), F32), pltpu.VMEM((NJ, 8, NK), F32)],
        in_specs=[SM, ANY],
        out_specs=[VM] * 2,
        scratch_shapes=[
            pltpu.VMEM((2, 2, LN, 8, HALF), F32),
            pltpu.VMEM((2, NV, NJ, HALF), F32),
            pltpu.SemaphoreType.DMA((2 + NV, 2)),
        ],
        compiler_params=params(4),
        name="begin",
    )(edge, state)


def halves(x):
    top = x.astype(BF16)
    return top, (x - top.astype(F32)).astype(BF16)


def shifted(x):
    half = NK // 2
    a, b = x[:, :half], x[:, half:]
    lane = iota(a.shape, 1)
    first, end = lane == 0, lane == half - 1
    ra, rb = pltpu.roll(a, 1, 1), pltpu.roll(b, 1, 1)
    la, lb = pltpu.roll(a, half - 1, 1), pltpu.roll(b, half - 1, 1)
    zero = jnp.zeros_like(a)
    left = jnp.where(first, zero, ra) + jnp.where(end, lb, la)
    right = jnp.where(first, ra, rb) + jnp.where(end, zero, lb)
    return jnp.concatenate([left, right], axis=1)


def fetches(pairs, sems):
    def copies(step, slot):
        rows = pl.ds(step * BLOCK, BLOCK)
        return [
            pltpu.make_async_copy(array.at[:, rows, lanes(h)], place(step, slot, h), sems.at[n, h, slot])
            for n, (array, place) in enumerate(pairs)
            for h in range(2)
        ]

    def start(step, slot):
        for copy in copies(step, slot):
            copy.start()

    def wait(step, slot):
        for copy in copies(step, slot):
            copy.wait()

    return start, wait


def joined(ref, at, count, stride, v):
    parts = []
    for h in range(2):
        half = ref.at[h].reshape(ref.shape[1] * ref.shape[2], HALF)
        parts.append(half[pl.ds(at + v * count * stride, count, stride=stride), :])
    return jnp.concatenate(parts, axis=1)


def relax(row, s_buf, d_buf, weights, out, stack):
    def gather(step, slot):
        for n in range(BLOCK):
            d = joined(d_buf.at[slot], n, NI, BLOCK, 0)
            for v in range(NV):
                s = row(step, n, v)
                if n == 0:
                    below = row(jnp.maximum(step - 1, 0), BLOCK - 1, v) * jnp.where(step == 0, 0.0, 1.0)
                else:
                    below = row(step, n - 1, v)
                if n == BLOCK - 1:
                    above = row(jnp.minimum(step + 1, STEPS - 1), 0, v) * jnp.where(step == STEPS - 1, 0.0, 1.0)
                else:
                    above = row(step, n + 1, v)
                e = joined(s_buf.at[slot], n, NI, BLOCK, v) - d * s + (below + above) + shifted(s)
                e_hi, e_lo = halves(e)
                s_hi, s_lo = halves(s)
                for k, part in enumerate((e_hi, e_lo, s_hi, s_lo)):
                    stack[slot, n, k * LN + v * NI : k * LN + (v + 1) * NI] = part

    def solve(step, slot):
        for n in range(BLOCK):
            both = mul(weights[...], stack[slot, n])
            for v in range(NV):
                at = v * NI
                change = both[at : at + NI] + both[LN + at : LN + at + NI]
                out[step * BLOCK + n, at : at + NI] = row(step, n, v) + change

    return gather, solve


def blend_ghosts(coef, window, j):
    total = coef[j, 0] * window[j]
    for d in range(1, 5):
        total = total + coef[j, d] * window[j + d]
    g_hi = high_part(total)
    g_lo = high_part(total - g_hi)
    return jnp.concatenate([g_hi, g_lo, g_hi, jnp.zeros_like(g_hi)], axis=0).astype(BF16)


def fill_window(window, lo, hi, plane):
    window[0:2] = lo[...]
    window[2 : NJ + 2] = plane[...]
    window[NJ + 2 :] = hi[...]


def turned_face(face, stack, face_w, flip_w):
    f_hi, f_lo = halves(face[...])
    stack[:LN] = f_hi
    stack[LN:] = f_lo
    both = mul(face_w[...], mul(stack[...], flip_w[...]).astype(BF16))
    return both[:LN] + both[LN:]


def interior_kernel(state, source, diagonal, weights, out, stack, s_buf, d_buf, sems, held, more):
    start, wait = fetches(
        [
            (source, lambda step, slot, h: s_buf.at[slot, h]),
            (diagonal, lambda step, slot, h: d_buf.at[slot, h]),
        ],
        sems,
    )

    def load(step):
        rows = pl.ds(step * BLOCK, BLOCK)
        return [
            pltpu.make_async_copy(state.at[:, rows, lanes(h)], held.at[step, h], more.at[h, step])
            for h in range(2)
        ]

    def arrived(step):
        for copy in load(step):
            copy.wait()

    def row(step, n, v):
        return joined(held.at[step], n, NI, BLOCK, v)

    gather, solve = relax(row, s_buf, d_buf, weights, out, stack)
    for step in range(STEPS):
        for copy in load(step):
            copy.start()
        if step < 2:
            start(step, step)
    arrived(0)
    arrived(1)
    wait(0, 0)
    gather(0, 0)
    wait(1, 1)

    def pair(step, carry):
        first = 2 * step

        @pl.when(first + 2 < STEPS)
        def _():
            start(first + 2, 0)
            arrived(first + 2)

        gather(first + 1, 1)
        solve(first, 0)

        @pl.when(first + 2 < STEPS)
        def _():
            start(first + 3, 1)
            arrived(first + 3)
            wait(first + 2, 0)

        gather(jnp.minimum(first + 2, STEPS - 1), 0)
        solve(first + 1, 1)

        @pl.when(first + 2 < STEPS)
        def _():
            wait(first + 3, 1)

        return carry

    lax.fori_loop(0, STEPS // 2, pair, 0)


RELAX_SCRATCH = [
    pltpu.VMEM((2, BLOCK, 4 * LN, NK), BF16),
    pltpu.VMEM((2, 2, LN, BLOCK, HALF), F32),
    pltpu.VMEM((2, 2, NI, BLOCK, HALF), F32),
    pltpu.SemaphoreType.DMA((2, 2, 2)),
]
RELAX_COST = pl.CostEstimate(flops=4_800_000_000, bytes_accessed=14_000_000, transcendentals=0)


def interior(state, source, diagonal, weights):
    return pl.pallas_call(
        interior_kernel,
        out_shape=pltpu.VMEM((NJ, LN, NK), F32),
        in_specs=[ANY, ANY, ANY, VM],
        out_specs=VM,
        scratch_shapes=RELAX_SCRATCH
        + [pltpu.VMEM((STEPS, 2, LN, BLOCK, HALF), F32), pltpu.SemaphoreType.DMA((2, STEPS))],
        compiler_params=params(16),
        cost_estimate=RELAX_COST,
        name="interior",
    )(state, source, diagonal, weights)


def advance_kernel(part, ghosts, faces, source, diagonal, weights, ghost_w, out, stack, s_buf, d_buf, sems, fresh):
    start, wait = fetches(
        [
            (source, lambda step, slot, h: s_buf.at[slot, h]),
            (diagonal, lambda step, slot, h: d_buf.at[slot, h]),
        ],
        sems,
    )

    def fix(step):
        for n in range(BLOCK):
            j = step * BLOCK + n
            value = part[j] + mul(ghost_w[...], ghosts[j])
            if n == BLOCK - 1:
                value = jnp.where(j == NJ - 1, faces[1], value)
            fresh[j] = value

    def row(step, n, v):
        return fresh[step * BLOCK + n, v * NI : (v + 1) * NI]

    gather, solve = relax(row, s_buf, d_buf, weights, out, stack)
    start(0, 0)
    start(1, 1)
    for step in range(3):
        fix(step)
    fresh[0] = faces[0]
    wait(0, 0)
    gather(0, 0)
    wait(1, 1)

    def pair(step, carry):
        first = 2 * step

        @pl.when(first + 2 < STEPS)
        def _():
            start(first + 2, 0)

        fix(jnp.minimum(first + 3, STEPS - 1))
        gather(first + 1, 1)
        solve(first, 0)

        @pl.when(first + 2 < STEPS)
        def _():
            start(first + 3, 1)
            wait(first + 2, 0)

        fix(jnp.minimum(first + 4, STEPS - 1))
        gather(jnp.minimum(first + 2, STEPS - 1), 0)
        solve(first + 1, 1)

        @pl.when(first + 2 < STEPS)
        def _():
            wait(first + 3, 1)

        return carry

    lax.fori_loop(0, STEPS // 2, pair, 0)


def advance(part, ghosts, faces, source, diagonal, weights, ghost_w):
    return pl.pallas_call(
        advance_kernel,
        out_shape=pltpu.VMEM((NJ, LN, NK), F32),
        in_specs=[VM, VM, VM, ANY, ANY, VM, VM],
        out_specs=VM,
        scratch_shapes=RELAX_SCRATCH + [pltpu.VMEM((NJ, LN, NK), F32)],
        compiler_params=params(16),
        cost_estimate=RELAX_COST,
        name="advance",
    )(part, ghosts, faces, source, diagonal, weights, ghost_w)


def border_kernel(
    coef, edge, part, plane, lo, hi, faces, ghost_w, edge_w, face_w, flip_w,
    ghosts, face_out, plane_out, window, stack,
):
    fill_window(window, lo, hi, plane)
    at = edge[0]

    def block(step, carry):
        for n in range(BLOCK):
            j = step * BLOCK + n
            g = blend_ghosts(coef, window, j)
            ghosts[j] = g
            rows = [part[j, pl.ds(v * NI + at, 1), :] for v in range(NV)]
            old = jnp.concatenate(rows + [jnp.zeros((2, NK), F32)], axis=0)
            plane_out[j] = old + mul(edge_w[...], g)[:8]
        return carry

    lax.fori_loop(0, STEPS, block, 0)
    for side, j in ((0, 0), (1, NJ - 1)):
        change = turned_face(faces.at[1 - side], stack, face_w, flip_w)
        face_out[side] = part[j] + mul(ghost_w[...], ghosts[j]) + change
        rows = [face_out[side, pl.ds(v * NI + at, 1), :] for v in range(NV)]
        plane_out[j] = jnp.concatenate(rows + [jnp.zeros((2, NK), F32)], axis=0)


def border(coef, edge, part, plane, lo, hi, faces, ghost_w, edge_w, face_w, flip_w):
    return pl.pallas_call(
        border_kernel,
        out_shape=[
            pltpu.VMEM((NJ, 32, NK), BF16),
            pltpu.VMEM((2, LN, NK), F32),
            pltpu.VMEM((NJ, 8, NK), F32),
        ],
        in_specs=[SM, SM] + [VM] * 9,
        out_specs=[VM] * 3,
        scratch_shapes=[pltpu.VMEM((NJ + 4, 8, NK), F32), pltpu.VMEM((2 * LN, NK), BF16)],
        compiler_params=params(4),
        name="border",
    )(coef, edge, part, plane, lo, hi, faces, ghost_w, edge_w, face_w, flip_w)


def finish_kernel(
    coef, part, plane, lo, hi, faces, ghost_w, face_w, flip_w, out, window, stack, held, sems
):
    fill_window(window, lo, hi, plane)

    def copies(step, slot):
        rows = pl.ds(step * BLOCK, BLOCK)
        return [
            pltpu.make_async_copy(held.at[slot, h], out.at[:, rows, lanes(h)], sems.at[slot, h])
            for h in range(2)
        ]

    def keep(slot, n, value):
        for h in range(2):
            half = held.at[slot, h].reshape(LN * BLOCK, HALF)
            half[pl.ds(n, LN, stride=BLOCK), :] = value[:, h * HALF : (h + 1) * HALF]

    for step in range(STEPS):
        slot = step % 2
        if step >= 2:
            for copy in copies(step - 2, slot):
                copy.wait()
        for n in range(BLOCK):
            j = step * BLOCK + n
            value = part[j] + mul(ghost_w[...], blend_ghosts(coef, window, j))
            if j == 0:
                value = value + turned_face(faces.at[1], stack, face_w, flip_w)
            if j == NJ - 1:
                value = value + turned_face(faces.at[0], stack, face_w, flip_w)
            keep(slot, n, value)
        for copy in copies(step, slot):
            copy.start()
    for step in range(STEPS - 2, STEPS):
        for copy in copies(step, step % 2):
            copy.wait()


def finish(coef, part, plane, lo, hi, faces, ghost_w, face_w, flip_w):
    return pl.pallas_call(
        finish_kernel,
        out_shape=jax.ShapeDtypeStruct((LN, NJ, NK), F32),
        in_specs=[SM] + [VM] * 8,
        out_specs=ANY,
        scratch_shapes=[
            pltpu.VMEM((NJ + 4, 8, NK), F32),
            pltpu.VMEM((2 * LN, NK), BF16),
            pltpu.VMEM((2, 2, LN, BLOCK, HALF), F32),
            pltpu.SemaphoreType.DMA((2, 2)),
        ],
        compiler_params=params(8),
        name="finish",
    )(coef, part, plane, lo, hi, faces, ghost_w, face_w, flip_w)


def exchange(faces, plane, bit, blocks):
    def across(step):
        return [
            (r * blocks + b, (1 - r) * blocks + (b + step) % blocks)
            for r in range(2)
            for b in range(blocks)
        ]

    axes = ("row", "blk")
    other = lax.ppermute(plane, "row", [(0, 1), (1, 0)])
    lo = lax.ppermute(plane[NJ - 2 :], axes, across(1))
    hi = lax.ppermute(plane[:2], axes, across(-1))
    got = [lax.ppermute(faces, "blk", [(b, b ^ (1 << k)) for b in range(blocks)]) for k in range(3)]
    received = jnp.where(bit == 0, got[0], jnp.where(bit == 1, got[1], got[2]))
    return other, lo, hi, received


def body(flow_state, forcing, stiffness, advection, line_inverse, margin_rows, margin_weights, partner_bit, turn_code):
    blocks = lax.axis_size("blk")
    row = lax.axis_index("row")
    bit = partner_bit[0, 0]
    state = in_hbm(flow_state.reshape(LN, NJ, NK))
    source = in_hbm(forcing.reshape(LN, NJ, NK))
    diagonal = in_hbm(stiffness.reshape(NI, NJ, NK))
    edge = jnp.where(row == 0, NI - 1, 0).reshape(1)
    comm = exchange(*begin(edge, state), bit, blocks)
    slots = margin_rows[0, 0] - jnp.arange(NJ, dtype=jnp.int32)[:, None]
    coef = jnp.sum(
        jnp.where(slots[..., None] == jnp.arange(5, dtype=jnp.int32), margin_weights[0, 0][..., None], 0.0), axis=1
    )
    flags = jnp.stack([row, turn_code[0, 0]])
    jac = jnp.pad(advection[0, 0], ((0, 2), (0, 2)))
    sweep_w, ghost_w, edge_w, face_w, flip_w = prepare(flags, line_inverse[0, 0], jac)
    sweep_w, coef = lax.optimization_barrier((sweep_w, coef))
    part = interior(state, source, diagonal, sweep_w)
    for sweep in range(SWEEPS - 1):
        ghosts, faces, plane = border(coef, edge, part, *comm, ghost_w, edge_w, face_w, flip_w)
        comm = exchange(faces, plane, bit, blocks)
        part = advance(part, ghosts, faces, source, diagonal, sweep_w, ghost_w)
    out = finish(coef, part, *comm, ghost_w, face_w, flip_w)
    return out.reshape(flow_state.shape)


def solution(mesh):
    return jax.shard_map(
        body,
        mesh=mesh,
        in_specs=(P("row", "blk"),) * 9,
        out_specs=P("row", "blk"),
        check_vma=False,
    )
```

time: 137 us -> 99.8 us (0.73)
  local copies, waits for them, and re-layouts: 39.1 us -> 5.62 us
  Pallas kernels: 48.9 us -> 46.4 us
    unnamed x33 -> x15, local copies, waits for them, and re-layouts: 32.6 us -> 5.51 us
    pallas_call x3 -> x1, Pallas kernels: 27.1 us -> 11.3 us  [interior(): pl.pallas_call(interior_kernel, out_shape=pltpu.VMEM((NJ, LN, NK), F32),...]
    pallas_call x3 -> x6, Pallas kernels: 19.8 us -> 33.1 us  [the longest x2 18.8 us: advance(): pl.pallas_call(advance_kernel, out_shape=pltpu.VMEM((NJ, LN, NK), F32), i...]
    another operation x1 -> x0, local copies, waits for them, and re-layouts: 6.28 us -> none  [body(): return state.transpose(1, 0, 2).reshape(field.shape)[None, None]]
    ppermute x3, starting transfers between devices: 10.6 us -> 9.05 us  [exchange(): hi = lax.ppermute(plane[:2], axes, across(-1))]
  transfers between devices with their start and end apart: 18 -> 18, of which waited for: 5 -> 5; matrix products, arithmetic and copies ran while one was open for 9% -> 0% of each run, Pallas kernels for 21% -> 32%
where the time goes in v2:
time: 99.8 us; the launch traced here: 99.2 us
  Pallas kernels  46.4 us (46%)
  waiting for transfers between devices  25.4 us (25%)
  starting transfers between devices  19.9 us (20%)
  local copies, waits for them, and re-layouts  5.62 us (6%)
  between operations  1.72 us (2%)
    ppermute x3, waiting for transfers between devices, exchange(): lo = lax.ppermute(plane[NJ - 2:], axes, across(1))  23.2 us
    pallas_call x2, Pallas kernels, advance(): pl.pallas_call(advance_kernel, out_shape=pltpu.VMEM((NJ, LN, NK), F32), i...  18.8 us
    pallas_call x1, Pallas kernels, interior(): pl.pallas_call(interior_kernel, out_shape=pltpu.VMEM((NJ, LN, NK), F32),...  11.3 us
    ppermute x3, starting transfers between devices, exchange(): hi = lax.ppermute(plane[:2], axes, across(-1))  9.05 us
    ppermute x9, starting transfers between devices, exchange(): lax.ppermute(faces, 'blk', [(b, b ^ 1 << k) for b in range(blocks)])  7.35 us
    pallas_call x1, Pallas kernels, finish(): pl.pallas_call(finish_kernel, out_shape=jax.ShapeDtypeStruct((LN, NJ, NK)...  6.57 us
    pallas_call x2, Pallas kernels, border(): pl.pallas_call(border_kernel, out_shape=[pltpu.VMEM((NJ, 32, NK), BF16),...  5.8 us
    unnamed x15, local copies, waits for them, and re-layouts  5.51 us
  transfers between devices with their start and end apart: 18, of which 5 were waited for; matrix products, arithmetic and copies ran while one was open for 0% of the time, Pallas kernels for 32%

profile of v2, /device:TPU:1, one launch (start us, length us, event | category | flops | bytes accessed | tf_op | source)
XLA Modules:
  0.0 99.2 jit_solution(11937512033174297942)
XLA Ops:
  0.0 1.9 %begin.1 = (f32[2,96,256]{2,1,0:T(8,128)S(1)}, f32[64,8,256]{2,1,0:T(8,128)S(1)}) custom-call(s32[1]{0:T(128)} %bitcast.8.edge, f32[96,64,256]{2,1,0:T(8,128)} %bitcast.21), custom_call_target="tpu_custom_call" | custom-call | tf_op jit(solution)/shard_map/begin/pallas_call | solution.py:159
  2.0 2.5 %collective-permute-start.5 = (f32[2,96,256]{2,1,0:T(8,128)S(1)}, f32[2,96,256]{2,1,0:T(8,128)S(1)}, u32[]{:S(2)}, u32[]{:S(2)}) collective-permute-start(f32[2,96,256]{2,1,0:T(8,128)S(1)} %get-tuple-element.24), channel_id=1, source_target_pairs={{0,4},{1,5},{2,6},{3,7},{4,0},{5,1},{6,2},{7,3},{8,12},{9,13},{10,... | collective-permute-start | bytes 589832 | tf_op jit(solution)/shard_map/ppermute | solution.py:540
  4.5 2.9 %collective-permute-start.4 = (f32[2,96,256]{2,1,0:T(8,128)S(1)}, f32[2,96,256]{2,1,0:T(8,128)S(1)}, u32[]{:S(2)}, u32[]{:S(2)}) collective-permute-start(f32[2,96,256]{2,1,0:T(8,128)S(1)} %get-tuple-element.24), channel_id=1, source_target_pairs={{0,2},{1,3},{2,0},{3,1},{4,6},{5,7},{6,4},{7,5},{8,10},{9,11},{10,... | collective-permute-start | bytes 589832 | tf_op jit(solution)/shard_map/ppermute | solution.py:540
  7.8 1.5 %collective-permute-start = (f32[64,8,256]{2,1,0:T(8,128)S(1)}, f32[64,8,256]{2,1,0:T(8,128)S(1)}, u32[]{:S(2)}, u32[]{:S(2)}) collective-permute-start(f32[64,8,256]{2,1,0:T(8,128)S(1)} %get-tuple-element.23), channel_id=1, source_target_pairs={{0,64},{64,0},{1,65},{65,1},{2,66},{66,2},{3,67},{67,3},{4,68},{68... | collective-permute-start | bytes 1572872 | tf_op jit(solution)/shard_map/ppermute | solution.py:537
  9.4 4.2 %collective-permute-start.2 = (f32[2,8,256]{2,1,0:T(8,128)S(1)}, f32[2,8,256]{2,1,0:T(8,128)S(1)}, u32[]{:S(2)}, u32[]{:S(2)}) collective-permute-start(f32[2,8,256]{2,1,0:T(8,128)S(1)} %get-tuple-element.39), channel_id=1, source_target_pairs={{0,127},{1,64},{2,65},{3,66},{4,67},{5,68},{6,69},{7,70},{8,71},{9... | collective-permute-start | bytes 49160 | tf_op jit(solution)/shard_map/ppermute | solution.py:539
  14.4 2.0 %prepare.1 = (bf16[192,384]{1,0:T(8,128)(2,1)S(1)}, bf16[96,32]{1,0:T(8,128)(2,1)S(1)}, bf16[16,32]{1,0:T(8,128)(2,1)S(1)}, bf16[192,192]{1,0:T(8,128)(2,1)S(1)}, bf16[256,256]{1,0:T(8,128)(2,1)S(1)}) custom-call(s32[2]{0:T(128)S(1)} %pad_add_fusion.flags, f32[96,96]{1,0:T(8,128)S(1)} %bitcast.17, f32[8,8]{1,0:T(8,128)S(1)} %pad.4.jacobian), custom_call_target="tpu_custom_call" | custom-call | tf_op jit(solution)/shard_map/prepare/pallas_call | solution.py:113
  16.4 11.3 %interior.1.part = f32[64,96,256]{2,1,0:T(8,128)S(1)} custom-call(f32[96,64,256]{2,1,0:T(8,128)} %bitcast.22, f32[96,64,256]{2,1,0:T(8,128)} %bitcast.18, f32[16,64,256]{2,1,0:T(8,128)} %bitcast.23, bf16[192,384]{1,0:T(8,128)(2,1)S(1)} %get-tuple-element.22.weights), custom_call_target="tpu_custom_call" | custom-call | flops 4800000000 | bytes 14000000 | tf_op jit(solution)/shard_map/interior/pallas_call | solution.py:348
  27.8 2.7 %copy-done = f32[64,96,256]{2,1,0:T(8,128)} copy-done((f32[64,96,256]{2,1,0:T(8,128)}, f32[64,96,256]{2,1,0:T(8,128)S(1)}, u32[]{:S(2)}) %copy-start) | copy-done | bytes 6291480
  31.4 8.5 %collective-permute-done.1.lo = f32[2,8,256]{2,1,0:T(8,128)S(1)} collective-permute-done((f32[2,8,256]{2,1,0:T(8,128)S(1)}, f32[2,8,256]{2,1,0:T(8,128)S(1)}, u32[]{:S(2)}, u32[]{:S(2)}) %collective-permute-start.1) | collective-permute-done | bytes 16416 | tf_op jit(solution)/shard_map/ppermute | solution.py:538
  39.9 2.8 %copy-done.1 = f32[64,96,256]{2,1,0:T(8,128)S(1)} copy-done((f32[64,96,256]{2,1,0:T(8,128)S(1)}, f32[64,96,256]{2,1,0:T(8,128)}, u32[]{:S(2)}) %copy-start.1) | copy-done | bytes 6291480
  42.7 2.9 %border.2 = (bf16[64,32,256]{2,1,0:T(8,128)(2,1)S(1)}, f32[2,96,256]{2,1,0:T(8,128)S(1)}, f32[64,8,256]{2,1,0:T(8,128)S(1)}) custom-call(f32[64,5]{1,0:T(8,128)S(1)} %copy.14.coef, s32[1]{0:T(128)} %bitcast.8.edge, f32[64,96,256]{2,1,0:T(8,128)S(1)} %copy-done.1, f32[64,8,256]{2,1,0:T(8,128)S(1)} %collective-permute-done.plane, ...), custom_call_target="tpu_custom_call" | custom-call | tf_op jit(solution)/shard_map/border/pallas_call | solution.py:459
  46.4 9.4 %advance.2.part = f32[64,96,256]{2,1,0:T(8,128)S(1)} custom-call(f32[64,96,256]{2,1,0:T(8,128)S(1)} %copy-done.2, bf16[64,32,256]{2,1,0:T(8,128)(2,1)S(1)} %get-tuple-element.29.ghosts, f32[2,96,256]{2,1,0:T(8,128)S(1)} %get-tuple-element.30.faces, f32[96,64,256]{2,1,0:T(8,128)} %bitcast.19, f32[16,64,256]{2,1,0:T(8,128)} %bitcast.24, ...), custom_call_target="tpu_custom_call" | custom-call | flops 4800000000 | bytes 14000000 | tf_op jit(solution)/shard_map/advance/pallas_call | solution.py:421
  55.8 1.3 %collective-permute-start.8 = (f32[2,8,256]{2,1,0:T(8,128)S(1)}, f32[2,8,256]{2,1,0:T(8,128)S(1)}, u32[]{:S(2)}, u32[]{:S(2)}) collective-permute-start(f32[2,8,256]{2,1,0:T(8,128)S(1)} %get-tuple-element.37), channel_id=1, source_target_pairs={{0,127},{1,64},{2,65},{3,66},{4,67},{5,68},{6,69},{7,70},{8,71},{9... | collective-permute-start | bytes 49160 | tf_op jit(solution)/shard_map/ppermute | solution.py:539
  57.1 0.5 collective-permute-start.7
  57.7 1.4 %collective-permute-done.8.hi = f32[2,8,256]{2,1,0:T(8,128)S(1)} collective-permute-done((f32[2,8,256]{2,1,0:T(8,128)S(1)}, f32[2,8,256]{2,1,0:T(8,128)S(1)}, u32[]{:S(2)}, u32[]{:S(2)}) %collective-permute-start.8) | collective-permute-done | bytes 16416 | tf_op jit(solution)/shard_map/ppermute | solution.py:539
  59.0 6.8 %collective-permute-done.7.lo = f32[2,8,256]{2,1,0:T(8,128)S(1)} collective-permute-done((f32[2,8,256]{2,1,0:T(8,128)S(1)}, f32[2,8,256]{2,1,0:T(8,128)S(1)}, u32[]{:S(2)}, u32[]{:S(2)}) %collective-permute-start.7) | collective-permute-done | bytes 16416 | tf_op jit(solution)/shard_map/ppermute | solution.py:538
  65.8 2.9 %border.3 = (bf16[64,32,256]{2,1,0:T(8,128)(2,1)S(1)}, f32[2,96,256]{2,1,0:T(8,128)S(1)}, f32[64,8,256]{2,1,0:T(8,128)S(1)}) custom-call(f32[64,5]{1,0:T(8,128)S(1)} %copy.14.coef, s32[1]{0:T(128)} %bitcast.8.edge, f32[64,96,256]{2,1,0:T(8,128)S(1)} %advance.2.part, f32[64,8,256]{2,1,0:T(8,128)S(1)} %collective-permute-done.6.plane, ...), custom_call_target="tpu_custom_call" | custom-call | tf_op jit(solution)/shard_map/border/pallas_call | solution.py:459
  68.9 1.0 %collective-permute-start.15 = (f32[2,96,256]{2,1,0:T(8,128)S(1)}, f32[2,96,256]{2,1,0:T(8,128)S(1)}, u32[]{:S(2)}, u32[]{:S(2)}) collective-permute-start(f32[2,96,256]{2,1,0:T(8,128)S(1)} %get-tuple-element.33.faces), channel_id=1, source_target_pairs={{0,1},{1,0},{2,3},{3,2},{4,5},{5,4},{6,7},{7,6},{8,9},{9,8},{10,11... | collective-permute-start | bytes 589832 | tf_op jit(solution)/shard_map/ppermute | solution.py:540
  70.0 0.9 collective-permute-start.12
  70.9 9.4 %advance.3.part = f32[64,96,256]{2,1,0:T(8,128)S(1)} custom-call(f32[64,96,256]{2,1,0:T(8,128)S(1)} %advance.2.part, bf16[64,32,256]{2,1,0:T(8,128)(2,1)S(1)} %get-tuple-element.32.ghosts, f32[2,96,256]{2,1,0:T(8,128)S(1)} %get-tuple-element.33.faces, f32[96,64,256]{2,1,0:T(8,128)} %bitcast.20, f32[16,64,256]{2,1,0:T(8,128)} %bitcast.25, ...), custom_call_target="tpu_custom_call" | custom-call | flops 4800000000 | bytes 14000000 | tf_op jit(solution)/shard_map/advance/pallas_call | solution.py:421
  80.3 3.5 %collective-permute-start.14 = (f32[2,8,256]{2,1,0:T(8,128)S(1)}, f32[2,8,256]{2,1,0:T(8,128)S(1)}, u32[]{:S(2)}, u32[]{:S(2)}) collective-permute-start(f32[2,8,256]{2,1,0:T(8,128)S(1)} %get-tuple-element.35), channel_id=1, source_target_pairs={{0,127},{1,64},{2,65},{3,66},{4,67},{5,68},{6,69},{7,70},{8,71},{9... | collective-permute-start | bytes 49160 | tf_op jit(solution)/shard_map/ppermute | solution.py:539
  83.9 0.8 collective-permute-done.14.hi
  84.7 7.8 %collective-permute-done.13.lo = f32[2,8,256]{2,1,0:T(8,128)S(1)} collective-permute-done((f32[2,8,256]{2,1,0:T(8,128)S(1)}, f32[2,8,256]{2,1,0:T(8,128)S(1)}, u32[]{:S(2)}, u32[]{:S(2)}) %collective-permute-start.13) | collective-permute-done | bytes 16416 | tf_op jit(solution)/shard_map/ppermute | solution.py:538
  92.5 6.6 %finish.1 = f32[96,64,256]{2,1,0:T(8,128)} custom-call(f32[64,5]{1,0:T(8,128)S(1)} %copy.14.coef, f32[64,96,256]{2,1,0:T(8,128)S(1)} %advance.3.part, f32[64,8,256]{2,1,0:T(8,128)S(1)} %collective-permute-done.12.plane, f32[2,8,256]{2,1,0:T(8,128)S(1)} %collective-permute-done.13.lo, f32[2,8,256]{2,1,0:T(8,128)S(1)} %collective-permute-done.14.hi, ...), custom_call_target="tpu_custom_call" | custom-call | tf_op jit(solution)/shard_map/finish/pallas_call | solution.py:512
  (46 shorter events, 1.8 us)
Async XLA Ops:
  0.0 14.3 %copy-start.5 = (s32[1,1,64,4]{2,3,1,0:T(4,128)S(1)}, s32[1,1,64,4]{2,3,1,0:T(4,128)}, u32[]{:S(2)}) copy-start(s32[1,1,64,4]{2,3,1,0:T(4,128)} %param.14) | copy-start | bytes 3076
  0.0 14.3 %copy-start.4 = (f32[1,1,6,6]{3,1,2,0:T(1,128)S(1)}, f32[1,1,6,6]{3,1,2,0:T(1,128)}, u32[]{:S(2)}) copy-start(f32[1,1,6,6]{3,1,2,0:T(1,128)} %param.12) | copy-start | bytes 436
  0.0 14.4 %copy-start.6 = (f32[1,1,64,4]{2,3,1,0:T(4,128)S(1)}, f32[1,1,64,4]{2,3,1,0:T(4,128)}, u32[]{:S(2)}) copy-start(f32[1,1,64,4]{2,3,1,0:T(4,128)} %param.15) | copy-start | bytes 3076
  0.0 14.4 %copy-start.3 = (f32[1,1,96,96]{3,2,1,0:T(8,128)S(1)}, f32[1,1,96,96]{3,2,1,0:T(8,128)}, u32[]{:S(2)}) copy-start(f32[1,1,96,96]{3,2,1,0:T(8,128)} %param.13) | copy-start | bytes 110596
  2.0 29.2 %collective-permute-start.5 = (f32[2,96,256]{2,1,0:T(8,128)S(1)}, f32[2,96,256]{2,1,0:T(8,128)S(1)}, u32[]{:S(2)}, u32[]{:S(2)}) collective-permute-start(f32[2,96,256]{2,1,0:T(8,128)S(1)} %get-tuple-element.24), channel_id=1, source_target_pairs={{0,4},{1,5},{2,6},{3,7},{4,0},{5,1},{6,2},{7,3},{8,12},{9,13},{10,... | collective-permute-start | bytes 589832 | tf_op jit(solution)/shard_map/ppermute | solution.py:540
  4.5 26.8 %collective-permute-start.4 = (f32[2,96,256]{2,1,0:T(8,128)S(1)}, f32[2,96,256]{2,1,0:T(8,128)S(1)}, u32[]{:S(2)}, u32[]{:S(2)}) collective-permute-start(f32[2,96,256]{2,1,0:T(8,128)S(1)} %get-tuple-element.24), channel_id=1, source_target_pairs={{0,2},{1,3},{2,0},{3,1},{4,6},{5,7},{6,4},{7,5},{8,10},{9,11},{10,... | collective-permute-start | bytes 589832 | tf_op jit(solution)/shard_map/ppermute | solution.py:540
  7.4 23.9 %collective-permute-start.3 = (f32[2,96,256]{2,1,0:T(8,128)S(1)}, f32[2,96,256]{2,1,0:T(8,128)S(1)}, u32[]{:S(2)}, u32[]{:S(2)}) collective-permute-start(f32[2,96,256]{2,1,0:T(8,128)S(1)} %get-tuple-element.24), channel_id=1, source_target_pairs={{0,1},{1,0},{2,3},{3,2},{4,5},{5,4},{6,7},{7,6},{8,9},{9,8},{10,11... | collective-permute-start | bytes 589832 | tf_op jit(solution)/shard_map/ppermute | solution.py:540
  7.8 32.1 %collective-permute-start = (f32[64,8,256]{2,1,0:T(8,128)S(1)}, f32[64,8,256]{2,1,0:T(8,128)S(1)}, u32[]{:S(2)}, u32[]{:S(2)}) collective-permute-start(f32[64,8,256]{2,1,0:T(8,128)S(1)} %get-tuple-element.23), channel_id=1, source_target_pairs={{0,64},{64,0},{1,65},{65,1},{2,66},{66,2},{3,67},{67,3},{4,68},{68... | collective-permute-start | bytes 1572872 | tf_op jit(solution)/shard_map/ppermute | solution.py:537
  9.4 22.0 %collective-permute-start.2 = (f32[2,8,256]{2,1,0:T(8,128)S(1)}, f32[2,8,256]{2,1,0:T(8,128)S(1)}, u32[]{:S(2)}, u32[]{:S(2)}) collective-permute-start(f32[2,8,256]{2,1,0:T(8,128)S(1)} %get-tuple-element.39), channel_id=1, source_target_pairs={{0,127},{1,64},{2,65},{3,66},{4,67},{5,68},{6,69},{7,70},{8,71},{9... | collective-permute-start | bytes 49160 | tf_op jit(solution)/shard_map/ppermute | solution.py:539
  31.2 8.7 %collective-permute-start.1 = (f32[2,8,256]{2,1,0:T(8,128)S(1)}, f32[2,8,256]{2,1,0:T(8,128)S(1)}, u32[]{:S(2)}, u32[]{:S(2)}) collective-permute-start(f32[2,8,256]{2,1,0:T(8,128)S(1)} %get-tuple-element.40), channel_id=1, source_target_pairs={{0,65},{1,66},{2,67},{3,68},{4,69},{5,70},{6,71},{7,72},{8,73},{9,... | collective-permute-start | bytes 49160 | tf_op jit(solution)/shard_map/ppermute | solution.py:538
  39.9 2.8 %copy-start.1 = (f32[64,96,256]{2,1,0:T(8,128)S(1)}, f32[64,96,256]{2,1,0:T(8,128)}, u32[]{:S(2)}) copy-start(f32[64,96,256]{2,1,0:T(8,128)} %copy-done) | copy-start | bytes 18874372
  42.7 3.7 %copy-start.2 = (f32[64,96,256]{2,1,0:T(8,128)S(1)}, f32[64,96,256]{2,1,0:T(8,128)}, u32[]{:S(2)}) copy-start(f32[64,96,256]{2,1,0:T(8,128)} %copy-done) | copy-start | bytes 18874372
  45.6 11.5 %collective-permute-start.11 = (f32[2,96,256]{2,1,0:T(8,128)S(1)}, f32[2,96,256]{2,1,0:T(8,128)S(1)}, u32[]{:S(2)}, u32[]{:S(2)}) collective-permute-start(f32[2,96,256]{2,1,0:T(8,128)S(1)} %get-tuple-element.30.faces), channel_id=1, source_target_pairs={{0,4},{1,5},{2,6},{3,7},{4,0},{5,1},{6,2},{7,3},{8,12},{9,13},{10,... | collective-permute-start | bytes 589832 | tf_op jit(solution)/shard_map/ppermute | solution.py:540
  45.7 11.9 %collective-permute-start.10 = (f32[2,96,256]{2,1,0:T(8,128)S(1)}, f32[2,96,256]{2,1,0:T(8,128)S(1)}, u32[]{:S(2)}, u32[]{:S(2)}) collective-permute-start(f32[2,96,256]{2,1,0:T(8,128)S(1)} %get-tuple-element.30.faces), channel_id=1, source_target_pairs={{0,2},{1,3},{2,0},{3,1},{4,6},{5,7},{6,4},{7,5},{8,10},{9,11},{10,... | collective-permute-start | bytes 589832 | tf_op jit(solution)/shard_map/ppermute | solution.py:540
  45.8 11.8 %collective-permute-start.9 = (f32[2,96,256]{2,1,0:T(8,128)S(1)}, f32[2,96,256]{2,1,0:T(8,128)S(1)}, u32[]{:S(2)}, u32[]{:S(2)}) collective-permute-start(f32[2,96,256]{2,1,0:T(8,128)S(1)} %get-tuple-element.30.faces), channel_id=1, source_target_pairs={{0,1},{1,0},{2,3},{3,2},{4,5},{5,4},{6,7},{7,6},{8,9},{9,8},{10,11... | collective-permute-start | bytes 589832 | tf_op jit(solution)/shard_map/ppermute | solution.py:540
  45.9 19.9 %collective-permute-start.6 = (f32[64,8,256]{2,1,0:T(8,128)S(1)}, f32[64,8,256]{2,1,0:T(8,128)S(1)}, u32[]{:S(2)}, u32[]{:S(2)}) collective-permute-start(f32[64,8,256]{2,1,0:T(8,128)S(1)} %get-tuple-element.31), channel_id=1, source_target_pairs={{0,64},{64,0},{1,65},{65,1},{2,66},{66,2},{3,67},{67,3},{4,68},{68... | collective-permute-start | bytes 1572872 | tf_op jit(solution)/shard_map/ppermute | solution.py:537
  55.8 3.3 %collective-permute-start.8 = (f32[2,8,256]{2,1,0:T(8,128)S(1)}, f32[2,8,256]{2,1,0:T(8,128)S(1)}, u32[]{:S(2)}, u32[]{:S(2)}) collective-permute-start(f32[2,8,256]{2,1,0:T(8,128)S(1)} %get-tuple-element.37), channel_id=1, source_target_pairs={{0,127},{1,64},{2,65},{3,66},{4,67},{5,68},{6,69},{7,70},{8,71},{9... | collective-permute-start | bytes 49160 | tf_op jit(solution)/shard_map/ppermute | solution.py:539
  57.1 8.7 %collective-permute-start.7 = (f32[2,8,256]{2,1,0:T(8,128)S(1)}, f32[2,8,256]{2,1,0:T(8,128)S(1)}, u32[]{:S(2)}, u32[]{:S(2)}) collective-permute-start(f32[2,8,256]{2,1,0:T(8,128)S(1)} %get-tuple-element.38), channel_id=1, source_target_pairs={{0,65},{1,66},{2,67},{3,68},{4,69},{5,70},{6,71},{7,72},{8,73},{9,... | collective-permute-start | bytes 49160 | tf_op jit(solution)/shard_map/ppermute | solution.py:538
  68.7 15.1 %collective-permute-start.17 = (f32[2,96,256]{2,1,0:T(8,128)S(1)}, f32[2,96,256]{2,1,0:T(8,128)S(1)}, u32[]{:S(2)}, u32[]{:S(2)}) collective-permute-start(f32[2,96,256]{2,1,0:T(8,128)S(1)} %get-tuple-element.33.faces), channel_id=1, source_target_pairs={{0,4},{1,5},{2,6},{3,7},{4,0},{5,1},{6,2},{7,3},{8,12},{9,13},{10,... | collective-permute-start | bytes 589832 | tf_op jit(solution)/shard_map/ppermute | solution.py:540
  68.9 14.9 %collective-permute-start.16 = (f32[2,96,256]{2,1,0:T(8,128)S(1)}, f32[2,96,256]{2,1,0:T(8,128)S(1)}, u32[]{:S(2)}, u32[]{:S(2)}) collective-permute-start(f32[2,96,256]{2,1,0:T(8,128)S(1)} %get-tuple-element.33.faces), channel_id=1, source_target_pairs={{0,2},{1,3},{2,0},{3,1},{4,6},{5,7},{6,4},{7,5},{8,10},{9,11},{10,... | collective-permute-start | bytes 589832 | tf_op jit(solution)/shard_map/ppermute | solution.py:540
  68.9 14.9 %collective-permute-start.15 = (f32[2,96,256]{2,1,0:T(8,128)S(1)}, f32[2,96,256]{2,1,0:T(8,128)S(1)}, u32[]{:S(2)}, u32[]{:S(2)}) collective-permute-start(f32[2,96,256]{2,1,0:T(8,128)S(1)} %get-tuple-element.33.faces), channel_id=1, source_target_pairs={{0,1},{1,0},{2,3},{3,2},{4,5},{5,4},{6,7},{7,6},{8,9},{9,8},{10,11... | collective-permute-start | bytes 589832 | tf_op jit(solution)/shard_map/ppermute | solution.py:540
  70.0 22.5 %collective-permute-start.12 = (f32[64,8,256]{2,1,0:T(8,128)S(1)}, f32[64,8,256]{2,1,0:T(8,128)S(1)}, u32[]{:S(2)}, u32[]{:S(2)}) collective-permute-start(f32[64,8,256]{2,1,0:T(8,128)S(1)} %get-tuple-element.34), channel_id=1, source_target_pairs={{0,64},{64,0},{1,65},{65,1},{2,66},{66,2},{3,67},{67,3},{4,68},{68... | collective-permute-start | bytes 1572872 | tf_op jit(solution)/shard_map/ppermute | solution.py:537
  80.3 4.4 %collective-permute-start.14 = (f32[2,8,256]{2,1,0:T(8,128)S(1)}, f32[2,8,256]{2,1,0:T(8,128)S(1)}, u32[]{:S(2)}, u32[]{:S(2)}) collective-permute-start(f32[2,8,256]{2,1,0:T(8,128)S(1)} %get-tuple-element.35), channel_id=1, source_target_pairs={{0,127},{1,64},{2,65},{3,66},{4,67},{5,68},{6,69},{7,70},{8,71},{9... | collective-permute-start | bytes 49160 | tf_op jit(solution)/shard_map/ppermute | solution.py:539
  83.8 8.7 %collective-permute-start.13 = (f32[2,8,256]{2,1,0:T(8,128)S(1)}, f32[2,8,256]{2,1,0:T(8,128)S(1)}, u32[]{:S(2)}, u32[]{:S(2)}) collective-permute-start(f32[2,8,256]{2,1,0:T(8,128)S(1)} %get-tuple-element.36), channel_id=1, source_target_pairs={{0,65},{1,66},{2,67},{3,68},{4,69},{5,70},{6,71},{7,72},{8,73},{9,... | collective-permute-start | bytes 49160 | tf_op jit(solution)/shard_map/ppermute | solution.py:538
  (1 other events, 2.7 us)

commit v3 on v2

--- a/solution.py
+++ b/solution.py
@@ -16,6 +16,7 @@
 ANY = pl.BlockSpec(memory_space=pltpu.HBM)
 HI = lax.Precision.HIGHEST
 BLOCK = 8
+REACH = 5
 STEPS = NJ // BLOCK
 
 
@@ -47,7 +48,9 @@
     return jnp.dot(a, b, preferred_element_type=F32)
 
 
-def prepare_kernel(flags, inverse, jacobian, sweep_w, ghost_w, edge_w, face_w, flip_w):
+def prepare_kernel(
+    flags, inverse, jacobian, slots, shares, sweep_w, ghost_w, edge_w, face_w, flip_w, coef
+):
     rotor = flags[0] == 0
     code = flags[1]
     lines = inverse[...]
@@ -80,7 +83,10 @@
         total = hot(m == k + starts[0])
         for start in starts[1:]:
             total = total + hot(m == k + start)
-        return total
+        return total.astype(BF16)
+
+    def put(matrix, where):
+        return mul(matrix.astype(BF16), where)
 
     def split(matrix):
         top = high_part(matrix)
@@ -90,26 +96,32 @@
     b_hi, b_lo = split(both)
     width = 4 * LN
     sweep_w[:LN] = (
-        dot_exact(l_hi, place(LN, width, (0, LN)))
-        + dot_exact(b_hi, place(LN, width, (2 * LN, 3 * LN)))
+        put(l_hi, place(LN, width, (0, LN))) + put(b_hi, place(LN, width, (2 * LN, 3 * LN)))
     ).astype(BF16)
     sweep_w[LN:] = (
-        dot_exact(l_lo, place(LN, width, (0,))) + dot_exact(b_lo, place(LN, width, (2 * LN,)))
+        put(l_lo, place(LN, width, (0,))) + put(b_lo, place(LN, width, (2 * LN,)))
     ).astype(BF16)
     g_hi, g_lo = split(ghost)
-    full = dot_exact(g_hi, place(8, 32, (0, 8))) + dot_exact(g_lo, place(8, 32, (16,)))
+    full = put(g_hi, place(8, 32, (0, 8))) + put(g_lo, place(8, 32, (16,)))
     ghost_w[...] = full.astype(BF16)
-    pick = hot(jnp.logical_and(iota((16, LN), 1) == NI * iota((16, LN), 0) + edge, iota((16, LN), 0) < NV))
-    edge_w[...] = dot_exact(pick, full).astype(BF16)
+    at_edge = iota((16, LN), 1) == NI * iota((16, LN), 0) + edge
+    pick = hot(jnp.logical_and(at_edge, iota((16, LN), 0) < NV)).astype(BF16)
+    edge_w[...] = mul(pick, full.astype(BF16)).astype(BF16)
     f_hi, f_lo = split(face)
-    face_w[:LN] = dot_exact(f_hi, place(LN, 2 * LN, (0, LN))).astype(BF16)
-    face_w[LN:] = dot_exact(f_lo, place(LN, 2 * LN, (0,))).astype(BF16)
+    face_w[:LN] = put(f_hi, place(LN, 2 * LN, (0, LN))).astype(BF16)
+    face_w[LN:] = put(f_lo, place(LN, 2 * LN, (0,))).astype(BF16)
+    ones = jnp.ones((NJ, NK), F32)
+    diagonal = iota((NJ, NJ), 0) == iota((NJ, NJ), 1)
+    for d in range(REACH):
+        hits = slots[...] == iota(slots.shape, 1) + d
+        line = jnp.sum(jnp.where(hits, shares[...], 0.0), axis=0, keepdims=True)
+        coef[d] = dot_exact(jnp.where(diagonal, line, 0.0), ones)
     a, b = iota((NK, NK), 0), iota((NK, NK), 1)
     mirrored = hot(a + b == NK - 1)
     flip_w[...] = jnp.where(code // 2 == 1, mirrored, hot(a == b)).astype(BF16)
 
 
-def prepare(flags, inverse, jacobian):
+def prepare(flags, inverse, jacobian, slots, shares):
     return pl.pallas_call(
         prepare_kernel,
         out_shape=[
@@ -118,12 +130,13 @@
             pltpu.VMEM((16, 32), BF16),
             pltpu.VMEM((2 * LN, 2 * LN), BF16),
             pltpu.VMEM((NK, NK), BF16),
+            pltpu.VMEM((REACH, NJ, NK), F32),
         ],
-        in_specs=[SM, VM, VM],
-        out_specs=[VM] * 5,
+        in_specs=[SM, VM, VM, VM, VM],
+        out_specs=[VM] * 6,
         compiler_params=params(6),
         name="prepare",
-    )(flags, inverse, jacobian)
+    )(flags, inverse, jacobian, slots, shares)
 
 
 HALF = NK // 2
@@ -176,17 +189,15 @@
     return top, (x - top.astype(F32)).astype(BF16)
 
 
-def shifted(x):
-    half = NK // 2
-    a, b = x[:, :half], x[:, half:]
+def shifted(a, b):
     lane = iota(a.shape, 1)
-    first, end = lane == 0, lane == half - 1
+    first, end = lane == 0, lane == HALF - 1
     ra, rb = pltpu.roll(a, 1, 1), pltpu.roll(b, 1, 1)
-    la, lb = pltpu.roll(a, half - 1, 1), pltpu.roll(b, half - 1, 1)
+    la, lb = pltpu.roll(a, HALF - 1, 1), pltpu.roll(b, HALF - 1, 1)
     zero = jnp.zeros_like(a)
     left = jnp.where(first, zero, ra) + jnp.where(end, lb, la)
     right = jnp.where(first, ra, rb) + jnp.where(end, zero, lb)
-    return jnp.concatenate([left, right], axis=1)
+    return left, right
 
 
 def fetches(pairs, sems):
@@ -209,33 +220,33 @@
     return start, wait
 
 
-def joined(ref, at, count, stride, v):
-    parts = []
-    for h in range(2):
-        half = ref.at[h].reshape(ref.shape[1] * ref.shape[2], HALF)
-        parts.append(half[pl.ds(at + v * count * stride, count, stride=stride), :])
-    return jnp.concatenate(parts, axis=1)
+def spaced(ref, h, n, v):
+    half = ref.at[h].reshape(ref.shape[1] * BLOCK, HALF)
+    return half[pl.ds(n + v * NI * BLOCK, NI, stride=BLOCK), :]
 
 
 def relax(row, s_buf, d_buf, weights, out, stack):
     def gather(step, slot):
         for n in range(BLOCK):
-            d = joined(d_buf.at[slot], n, NI, BLOCK, 0)
+            d = [spaced(d_buf.at[slot], h, n, 0) for h in range(2)]
             for v in range(NV):
-                s = row(step, n, v)
-                if n == 0:
-                    below = row(jnp.maximum(step - 1, 0), BLOCK - 1, v) * jnp.where(step == 0, 0.0, 1.0)
-                else:
-                    below = row(step, n - 1, v)
-                if n == BLOCK - 1:
-                    above = row(jnp.minimum(step + 1, STEPS - 1), 0, v) * jnp.where(step == STEPS - 1, 0.0, 1.0)
-                else:
-                    above = row(step, n + 1, v)
-                e = joined(s_buf.at[slot], n, NI, BLOCK, v) - d * s + (below + above) + shifted(s)
-                e_hi, e_lo = halves(e)
-                s_hi, s_lo = halves(s)
-                for k, part in enumerate((e_hi, e_lo, s_hi, s_lo)):
-                    stack[slot, n, k * LN + v * NI : k * LN + (v + 1) * NI] = part
+                pair = [row(step, n, v, h) for h in range(2)]
+                along = shifted(*pair)
+                for h in range(2):
+                    s = pair[h]
+                    if n == 0:
+                        below = row(jnp.maximum(step - 1, 0), BLOCK - 1, v, h)
+                        below = below * jnp.where(step == 0, 0.0, 1.0)
+                    else:
+                        below = row(step, n - 1, v, h)
+                    if n == BLOCK - 1:
+                        above = row(jnp.minimum(step + 1, STEPS - 1), 0, v, h)
+                        above = above * jnp.where(step == STEPS - 1, 0.0, 1.0)
+                    else:
+                        above = row(step, n + 1, v, h)
+                    e = spaced(s_buf.at[slot], h, n, v) - d[h] * s + (below + above) + along[h]
+                    for k, value in enumerate(halves(e) + halves(s)):
+                        stack[slot, n, k * LN + v * NI : k * LN + (v + 1) * NI, lanes(h)] = value
 
     def solve(step, slot):
         for n in range(BLOCK):
@@ -243,15 +254,17 @@
             for v in range(NV):
                 at = v * NI
                 change = both[at : at + NI] + both[LN + at : LN + at + NI]
-                out[step * BLOCK + n, at : at + NI] = row(step, n, v) + change
+                for h in range(2):
+                    piece = change[:, h * HALF : (h + 1) * HALF]
+                    out[step * BLOCK + n, h, at : at + NI] = row(step, n, v, h) + piece
 
     return gather, solve
 
 
 def blend_ghosts(coef, window, j):
-    total = coef[j, 0] * window[j]
-    for d in range(1, 5):
-        total = total + coef[j, d] * window[j + d]
+    total = coef[0, pl.ds(j, 1), :] * window[j]
+    for d in range(1, REACH):
+        total = total + coef[d, pl.ds(j, 1), :] * window[j + d]
     g_hi = high_part(total)
     g_lo = high_part(total - g_hi)
     return jnp.concatenate([g_hi, g_lo, g_hi, jnp.zeros_like(g_hi)], axis=0).astype(BF16)
@@ -269,6 +282,9 @@
     stack[LN:] = f_lo
     both = mul(face_w[...], mul(stack[...], flip_w[...]).astype(BF16))
     return both[:LN] + both[LN:]
+
+
+PART = (NJ, 2, LN, HALF)
 
 
 def interior_kernel(state, source, diagonal, weights, out, stack, s_buf, d_buf, sems, held, more):
@@ -291,8 +307,8 @@
         for copy in load(step):
             copy.wait()
 
-    def row(step, n, v):
-        return joined(held.at[step], n, NI, BLOCK, v)
+    def row(step, n, v, h):
+        return spaced(held.at[step], h, n, v)
 
     gather, solve = relax(row, s_buf, d_buf, weights, out, stack)
     for step in range(STEPS):
@@ -347,7 +363,7 @@
 def interior(state, source, diagonal, weights):
     return pl.pallas_call(
         interior_kernel,
-        out_shape=pltpu.VMEM((NJ, LN, NK), F32),
+        out_shape=pltpu.VMEM(PART, F32),
         in_specs=[ANY, ANY, ANY, VM],
         out_specs=VM,
         scratch_shapes=RELAX_SCRATCH
@@ -370,20 +386,27 @@
     def fix(step):
         for n in range(BLOCK):
             j = step * BLOCK + n
-            value = part[j] + mul(ghost_w[...], ghosts[j])
-            if n == BLOCK - 1:
-                value = jnp.where(j == NJ - 1, faces[1], value)
-            fresh[j] = value
-
-    def row(step, n, v):
-        return fresh[step * BLOCK + n, v * NI : (v + 1) * NI]
+            change = mul(ghost_w[...], ghosts[j])
+            for h in range(2):
+                value = part[j, h] + change[:, h * HALF : (h + 1) * HALF]
+                if n == BLOCK - 1:
+                    value = jnp.where(j == NJ - 1, faces[1, :, lanes(h)], value)
+                fresh[j, h] = value
+
+    def row(step, n, v, h):
+        return fresh[step * BLOCK + n, h, v * NI : (v + 1) * NI]
 
     gather, solve = relax(row, s_buf, d_buf, weights, out, stack)
     start(0, 0)
     start(1, 1)
-    for step in range(3):
+
+    def early(step, carry):
         fix(step)
-    fresh[0] = faces[0]
+        return carry
+
+    lax.fori_loop(0, 3, early, 0)
+    for h in range(2):
+        fresh[0, h] = faces[0, :, lanes(h)]
     wait(0, 0)
     gather(0, 0)
     wait(1, 1)
@@ -420,10 +443,10 @@
 def advance(part, ghosts, faces, source, diagonal, weights, ghost_w):
     return pl.pallas_call(
         advance_kernel,
-        out_shape=pltpu.VMEM((NJ, LN, NK), F32),
+        out_shape=pltpu.VMEM(PART, F32),
         in_specs=[VM, VM, VM, ANY, ANY, VM, VM],
         out_specs=VM,
-        scratch_shapes=RELAX_SCRATCH + [pltpu.VMEM((NJ, LN, NK), F32)],
+        scratch_shapes=RELAX_SCRATCH + [pltpu.VMEM(PART, F32)],
         compiler_params=params(16),
         cost_estimate=RELAX_COST,
         name="advance",
@@ -432,27 +455,32 @@
 
 def border_kernel(
     coef, edge, part, plane, lo, hi, faces, ghost_w, edge_w, face_w, flip_w,
-    ghosts, face_out, plane_out, window, stack,
+    ghosts, face_out, plane_out, window, stack, kept,
 ):
     fill_window(window, lo, hi, plane)
     at = edge[0]
 
+    pad = jnp.zeros((2, HALF), F32)
+
     def block(step, carry):
-        for n in range(BLOCK):
-            j = step * BLOCK + n
+        for n in range(2 * BLOCK):
+            j = step * 2 * BLOCK + n
             g = blend_ghosts(coef, window, j)
             ghosts[j] = g
-            rows = [part[j, pl.ds(v * NI + at, 1), :] for v in range(NV)]
-            old = jnp.concatenate(rows + [jnp.zeros((2, NK), F32)], axis=0)
-            plane_out[j] = old + mul(edge_w[...], g)[:8]
+            change = mul(edge_w[...], g)
+            for h in range(2):
+                old = jnp.concatenate([part[j, h, pl.ds(at, NV, stride=NI), :], pad], axis=0)
+                plane_out[j, :, lanes(h)] = old + change[:8, h * HALF : (h + 1) * HALF]
         return carry
 
-    lax.fori_loop(0, STEPS, block, 0)
+    lax.fori_loop(0, STEPS // 2, block, 0)
     for side, j in ((0, 0), (1, NJ - 1)):
-        change = turned_face(faces.at[1 - side], stack, face_w, flip_w)
-        face_out[side] = part[j] + mul(ghost_w[...], ghosts[j]) + change
-        rows = [face_out[side, pl.ds(v * NI + at, 1), :] for v in range(NV)]
-        plane_out[j] = jnp.concatenate(rows + [jnp.zeros((2, NK), F32)], axis=0)
+        change = turned_face(faces.at[1 - side], stack, face_w, flip_w) + mul(ghost_w[...], ghosts[j])
+        for h in range(2):
+            kept[h] = part[j, h] + change[:, h * HALF : (h + 1) * HALF]
+            face_out[side, :, lanes(h)] = kept[h]
+            rows = jnp.concatenate([kept[h, pl.ds(at, NV, stride=NI), :], pad], axis=0)
+            plane_out[j, :, lanes(h)] = rows
 
 
 def border(coef, edge, part, plane, lo, hi, faces, ghost_w, edge_w, face_w, flip_w):
@@ -463,9 +491,13 @@
             pltpu.VMEM((2, LN, NK), F32),
             pltpu.VMEM((NJ, 8, NK), F32),
         ],
-        in_specs=[SM, SM] + [VM] * 9,
+        in_specs=[VM, SM] + [VM] * 9,
         out_specs=[VM] * 3,
-        scratch_shapes=[pltpu.VMEM((NJ + 4, 8, NK), F32), pltpu.VMEM((2 * LN, NK), BF16)],
+        scratch_shapes=[
+            pltpu.VMEM((NJ + 4, 8, NK), F32),
+            pltpu.VMEM((2 * LN, NK), BF16),
+            pltpu.VMEM((2, LN, HALF), F32),
+        ],
         compiler_params=params(4),
         name="border",
     )(coef, edge, part, plane, lo, hi, faces, ghost_w, edge_w, face_w, flip_w)
@@ -483,26 +515,36 @@
             for h in range(2)
         ]
 
-    def keep(slot, n, value):
+    def keep(slot, n, j, change):
         for h in range(2):
             half = held.at[slot, h].reshape(LN * BLOCK, HALF)
-            half[pl.ds(n, LN, stride=BLOCK), :] = value[:, h * HALF : (h + 1) * HALF]
-
-    for step in range(STEPS):
-        slot = step % 2
-        if step >= 2:
-            for copy in copies(step - 2, slot):
-                copy.wait()
-        for n in range(BLOCK):
-            j = step * BLOCK + n
-            value = part[j] + mul(ghost_w[...], blend_ghosts(coef, window, j))
-            if j == 0:
-                value = value + turned_face(faces.at[1], stack, face_w, flip_w)
-            if j == NJ - 1:
-                value = value + turned_face(faces.at[0], stack, face_w, flip_w)
-            keep(slot, n, value)
-        for copy in copies(step, slot):
-            copy.start()
+            half[pl.ds(n, LN, stride=BLOCK), :] = part[j, h] + change[:, h * HALF : (h + 1) * HALF]
+
+    first = turned_face(faces.at[1], stack, face_w, flip_w)
+    last = turned_face(faces.at[0], stack, face_w, flip_w)
+
+    def pair(step, carry):
+        for slot in range(2):
+            at = 2 * step + slot
+
+            @pl.when(step > 0)
+            def _():
+                for copy in copies(at - 2, slot):
+                    copy.wait()
+
+            for n in range(BLOCK):
+                j = at * BLOCK + n
+                change = mul(ghost_w[...], blend_ghosts(coef, window, j))
+                if n == 0 and slot == 0:
+                    change = change + first * jnp.where(step == 0, 1.0, 0.0)
+                if n == BLOCK - 1 and slot == 1:
+                    change = change + last * jnp.where(step == STEPS // 2 - 1, 1.0, 0.0)
+                keep(slot, n, j, change)
+            for copy in copies(at, slot):
+                copy.start()
+        return carry
+
+    lax.fori_loop(0, STEPS // 2, pair, 0)
     for step in range(STEPS - 2, STEPS):
         for copy in copies(step, step % 2):
             copy.wait()
@@ -512,7 +554,7 @@
     return pl.pallas_call(
         finish_kernel,
         out_shape=jax.ShapeDtypeStruct((LN, NJ, NK), F32),
-        in_specs=[SM] + [VM] * 8,
+        in_specs=[VM] * 9,
         out_specs=ANY,
         scratch_shapes=[
             pltpu.VMEM((NJ + 4, 8, NK), F32),
@@ -525,7 +567,7 @@
     )(coef, part, plane, lo, hi, faces, ghost_w, face_w, flip_w)
 
 
-def exchange(faces, plane, bit, blocks):
+def exchange(plane, blocks):
     def across(step):
         return [
             (r * blocks + b, (1 - r) * blocks + (b + step) % blocks)
@@ -537,9 +579,18 @@
     other = lax.ppermute(plane, "row", [(0, 1), (1, 0)])
     lo = lax.ppermute(plane[NJ - 2 :], axes, across(1))
     hi = lax.ppermute(plane[:2], axes, across(-1))
-    got = [lax.ppermute(faces, "blk", [(b, b ^ (1 << k)) for b in range(blocks)]) for k in range(3)]
-    received = jnp.where(bit == 0, got[0], jnp.where(bit == 1, got[1], got[2]))
-    return other, lo, hi, received
+    return other, lo, hi
+
+
+def beside(faces, bit, blocks, work, *operands):
+    def branch(k):
+        def run(faces, *operands):
+            received = lax.ppermute(faces, "blk", [(b, b ^ (1 << k)) for b in range(blocks)])
+            return received, work(*operands)
+
+        return run
+
+    return lax.switch(bit, [branch(k) for k in range(3)], faces, *operands)
 
 
 def body(flow_state, forcing, stiffness, advection, line_inverse, margin_rows, margin_weights, partner_bit, turn_code):
@@ -550,21 +601,23 @@
     source = in_hbm(forcing.reshape(LN, NJ, NK))
     diagonal = in_hbm(stiffness.reshape(NI, NJ, NK))
     edge = jnp.where(row == 0, NI - 1, 0).reshape(1)
-    comm = exchange(*begin(edge, state), bit, blocks)
-    slots = margin_rows[0, 0] - jnp.arange(NJ, dtype=jnp.int32)[:, None]
-    coef = jnp.sum(
-        jnp.where(slots[..., None] == jnp.arange(5, dtype=jnp.int32), margin_weights[0, 0][..., None], 0.0), axis=1
-    )
+    faces, plane = begin(edge, state)
+    comm = exchange(plane, blocks)
     flags = jnp.stack([row, turn_code[0, 0]])
     jac = jnp.pad(advection[0, 0], ((0, 2), (0, 2)))
-    sweep_w, ghost_w, edge_w, face_w, flip_w = prepare(flags, line_inverse[0, 0], jac)
-    sweep_w, coef = lax.optimization_barrier((sweep_w, coef))
-    part = interior(state, source, diagonal, sweep_w)
+    sweep_w, ghost_w, edge_w, face_w, flip_w, coef = prepare(
+        flags, line_inverse[0, 0], jac, margin_rows[0, 0].T, margin_weights[0, 0].T
+    )
+    received, part = beside(faces, bit, blocks, interior, state, source, diagonal, sweep_w)
     for sweep in range(SWEEPS - 1):
-        ghosts, faces, plane = border(coef, edge, part, *comm, ghost_w, edge_w, face_w, flip_w)
-        comm = exchange(faces, plane, bit, blocks)
-        part = advance(part, ghosts, faces, source, diagonal, sweep_w, ghost_w)
-    out = finish(coef, part, *comm, ghost_w, face_w, flip_w)
+        ghosts, faces, plane = border(
+            coef, edge, part, *comm, received, ghost_w, edge_w, face_w, flip_w
+        )
+        comm = exchange(plane, blocks)
+        received, part = beside(
+            faces, bit, blocks, advance, part, ghosts, faces, source, diagonal, sweep_w, ghost_w
+        )
+    out = finish(coef, part, *comm, received, ghost_w, face_w, flip_w)
     return out.reshape(flow_state.shape)
 
 

time: 99.8 us -> 73.6 us (0.74)
  waiting for transfers between devices: 25.4 us -> 0.03 us
  local copies, waits for them, and re-layouts: 5.62 us -> 0.03 us
  starting transfers between devices: 19.9 us -> 25.3 us
    ppermute x3, waiting for transfers between devices: 23.2 us -> 0.01 us  [exchange(): lo = lax.ppermute(plane[NJ - 2:], axes, across(1))]
    ppermute x3, starting transfers between devices: 9.05 us -> 22.8 us  [exchange(): hi = lax.ppermute(plane[:2], axes, across(-1))]
    ppermute x9 -> x3, starting transfers between devices: 7.35 us -> 0.09 us  [run(): lax.ppermute(faces, 'blk', [(b, b ^ 1 << k) for b in range(blocks)])]
    unnamed x15 -> x9, local copies, waits for them, and re-layouts: 5.51 us -> 0.02 us
    ppermute x3, waiting for transfers between devices: 2.17 us -> 0.01 us  [exchange(): hi = lax.ppermute(plane[:2], axes, across(-1))]
    pallas_call x2, Pallas kernels: 5.8 us -> 4.46 us  [border(): pl.pallas_call(border_kernel, out_shape=[pltpu.VMEM((NJ, 32, NK), BF16),...]
  transfers between devices with their start and end apart: 18 -> 12, of which waited for: 5 -> 0; matrix products, arithmetic and copies ran while one was open for 0% -> 0% of each run, Pallas kernels for 32% -> 45%
where the time goes in v3:
time: 73.6 us; the launch traced here: 73 us
  Pallas kernels  45.5 us (62%)
  starting transfers between devices  25.3 us (34%)
  between operations  1.7 us (2%)
    ppermute x3, starting transfers between devices, exchange(): hi = lax.ppermute(plane[:2], axes, across(-1))  22.8 us
    pallas_call x2, Pallas kernels, advance(): pl.pallas_call(advance_kernel, out_shape=pltpu.VMEM(PART, F32), in_specs=...  19.4 us
    pallas_call x1, Pallas kernels, interior(): pl.pallas_call(interior_kernel, out_shape=pltpu.VMEM(PART, F32), in_specs...  11.6 us
    pallas_call x1, Pallas kernels, finish(): pl.pallas_call(finish_kernel, out_shape=jax.ShapeDtypeStruct((LN, NJ, NK)...  6.49 us
    pallas_call x2, Pallas kernels, border(): pl.pallas_call(border_kernel, out_shape=[pltpu.VMEM((NJ, 32, NK), BF16),...  4.46 us
    ppermute x3, starting transfers between devices, exchange(): other = lax.ppermute(plane, 'row', [(0, 1), (1, 0)])  2.38 us
    pallas_call x1, Pallas kernels, begin(): pl.pallas_call(begin_kernel, out_shape=[pltpu.VMEM((2, LN, NK), F32), plt...  1.95 us
    pallas_call x1, Pallas kernels, prepare(): pl.pallas_call(prepare_kernel, out_shape=[pltpu.VMEM((2 * LN, 4 * LN), BF...  1.64 us
  transfers between devices with their start and end apart: 12, of which 0 were waited for; matrix products, arithmetic and copies ran while one was open for 0% of the time, Pallas kernels for 45%

profile of v3, /device:TPU:1, one launch (start us, length us, event | category | flops | bytes accessed | tf_op | source)
XLA Modules:
  0.0 73.0 jit_solution(7243850725952946682)
XLA Ops:
  0.0 1.9 %begin.1 = (f32[2,96,256]{2,1,0:T(8,128)S(1)}, f32[64,8,256]{2,1,0:T(8,128)S(1)}) custom-call(s32[1]{0:T(128)} %bitcast.8.edge, f32[96,64,256]{2,1,0:T(8,128)} %bitcast.22), custom_call_target="tpu_custom_call" | custom-call | tf_op jit(solution)/shard_map/begin/pallas_call | solution.py:172
  2.0 1.5 %collective-permute-start.9 = (f32[64,8,256]{2,1,0:T(8,128)S(1)}, f32[64,8,256]{2,1,0:T(8,128)S(1)}, u32[]{:S(2)}, u32[]{:S(2)}) collective-permute-start(f32[64,8,256]{2,1,0:T(8,128)S(1)} %get-tuple-element.200), channel_id=1, source_target_pairs={{0,64},{64,0},{1,65},{65,1},{2,66},{66,2},{3,67},{67,3},{4,68},{68... | collective-permute-start | bytes 1572872 | tf_op jit(solution)/shard_map/ppermute | solution.py:579
  3.5 8.5 %collective-permute-start.11 = (f32[2,8,256]{2,1,0:T(8,128)S(1)}, f32[2,8,256]{2,1,0:T(8,128)S(1)}, u32[]{:S(2)}, u32[]{:S(2)}) collective-permute-start(f32[2,8,256]{2,1,0:T(8,128)S(1)} %get-tuple-element.220), channel_id=1, source_target_pairs={{0,127},{1,64},{2,65},{3,66},{4,67},{5,68},{6,69},{7,70},{8,71},{9... | collective-permute-start | bytes 49160 | tf_op jit(solution)/shard_map/ppermute | solution.py:581
  12.0 0.0 collective-permute-start.10
  12.6 0.1 pad_add_fusion.flags
  13.4 1.6 %prepare.1 = (bf16[192,384]{1,0:T(8,128)(2,1)S(1)}, bf16[96,32]{1,0:T(8,128)(2,1)S(1)}, bf16[16,32]{1,0:T(8,128)(2,1)S(1)}, bf16[192,192]{1,0:T(8,128)(2,1)S(1)}...) custom-call(s32[2]{0:T(128)S(1)} %pad_add_fusion.flags, f32[96,96]{1,0:T(8,128)S(1)} %bitcast.19, ...), custom_call_target="tpu_custom_call" | custom-call | tf_op jit(solution)/shard_map/prepare/pallas_call | solution.py:125
  15.1 11.8 %conditional.3 = (f32[2,96,256]{2,1,0:T(8,128)}, f32[64,2,96,128]{3,2,1,0:T(8,128)S(1)}) conditional(s32[]{:T(128)} %bitcast.7, (f32[2,96,256]{2,1,0:T(8,128)S(1)}, f32[96,64,256]{2,1,0:T(8,128)}, f32[96,64,256]{2,1,0:T(8,128)}, f32[16,64,256]{2,1,0:T(8,128)}, bf16[192,384]{1,0:T(8,128)(2,1)S(1)}) %tuple.59, ...), branch_computations={%region_0.1_spmd, %region_1.2_spmd, %region_2.3_spmd} | conditional | flops 4800000000 | bytes 14786488 | solution.py:593
  15.1 0.1 collective-permute-start
  15.2 11.6 %interior.3 = f32[64,2,96,128]{3,2,1,0:T(8,128)S(1)} custom-call(f32[96,64,256]{2,1,0:T(8,128)} %get-tuple-element.120.state, f32[96,64,256]{2,1,0:T(8,128)} %get-tuple-element.121.source, f32[16,64,256]{2,1,0:T(8,128)} %get-tuple-element.122.diagonal, bf16[192,384]{1,0:T(8,128)(2,1)S(1)} %get-tuple-element.123.weights), custom_call_target="tpu_custom_call" | custom-call | flops 4800000000 | bytes 14000000 | tf_op jit(solution)/shard_map/cond/branch_0_fun/interior/pallas_call | solution.py:364
  26.8 0.0 collective-permute-done
  26.9 0.0 collective-permute-done.10.lo
  26.9 0.0 collective-permute-done.9.plane
  26.9 2.2 %border.2 = (bf16[64,32,256]{2,1,0:T(8,128)(2,1)S(1)}, f32[2,96,256]{2,1,0:T(8,128)S(1)}, f32[64,8,256]{2,1,0:T(8,128)S(1)}) custom-call(f32[5,64,256]{2,1,0:T(8,128)S(1)} %get-tuple-element.196.coef, s32[1]{0:T(128)} %bitcast.8.edge, f32[64,2,96,128]{3,2,1,0:T(8,128)S(1)} %get-tuple-element.199.part, f32[64,8,256]{2,1,0:T(8,128)S(1)} %collective-permute-done.9.plane, ...), custom_call_target="tpu_custom_call" | custom-call | tf_op jit(solution)/shard_map/border/pallas_call | solution.py:487
  29.1 0.7 collective-permute-start.12
  29.8 7.2 %collective-permute-start.14 = (f32[2,8,256]{2,1,0:T(8,128)S(1)}, f32[2,8,256]{2,1,0:T(8,128)S(1)}, u32[]{:S(2)}, u32[]{:S(2)}) collective-permute-start(f32[2,8,256]{2,1,0:T(8,128)S(1)} %get-tuple-element.218), channel_id=1, source_target_pairs={{0,127},{1,64},{2,65},{3,66},{4,67},{5,68},{6,69},{7,70},{8,71},{9... | collective-permute-start | bytes 49160 | tf_op jit(solution)/shard_map/ppermute | solution.py:581
  37.0 9.7 %conditional.4 = (f32[2,96,256]{2,1,0:T(8,128)}, f32[64,2,96,128]{3,2,1,0:T(8,128)S(1)}) conditional(s32[]{:T(128)} %bitcast.7, (f32[2,96,256]{2,1,0:T(8,128)S(1)}, f32[64,2,96,128]{3,2,1,0:T(8,128)S(1)}, bf16[64,32,256]{2,1,0:T(8,128)(2,1)S(1)}, f32[96,64,256]{2,1,0:T(8,128)}, f32[16,64,256]{2,1,0:T(8,128)}, ...), branch_computations={%region_3.4_spmd, %region_4.5_spmd, %region_5.6_spmd} | conditional | flops 4800000000 | bytes 14786488 | solution.py:593
  37.0 9.7 %advance.6 = f32[64,2,96,128]{3,2,1,0:T(8,128)S(1)} custom-call(f32[64,2,96,128]{3,2,1,0:T(8,128)S(1)} %get-tuple-element.135.part, bf16[64,32,256]{2,1,0:T(8,128)(2,1)S(1)} %get-tuple-element.136.ghosts, f32[2,96,256]{2,1,0:T(8,128)S(1)} %get-tuple-element.134.faces, f32[96,64,256]{2,1,0:T(8,128)} %get-tuple-element.137.source, ...), custom_call_target="tpu_custom_call" | custom-call | flops 4800000000 | bytes 14000000 | tf_op jit(solution)/shard_map/cond/branch_0_fun/advance/pallas_call | solution.py:444
  46.7 2.2 %border.3 = (bf16[64,32,256]{2,1,0:T(8,128)(2,1)S(1)}, f32[2,96,256]{2,1,0:T(8,128)S(1)}, f32[64,8,256]{2,1,0:T(8,128)S(1)}) custom-call(f32[5,64,256]{2,1,0:T(8,128)S(1)} %get-tuple-element.196.coef, s32[1]{0:T(128)} %bitcast.8.edge, f32[64,2,96,128]{3,2,1,0:T(8,128)S(1)} %get-tuple-element.208.part, f32[64,8,256]{2,1,0:T(8,128)S(1)} %collective-permute-done.12.plane, ...), custom_call_target="tpu_custom_call" | custom-call | tf_op jit(solution)/shard_map/border/pallas_call | solution.py:487
  49.0 0.2 collective-permute-start.15
  49.1 7.2 %collective-permute-start.17 = (f32[2,8,256]{2,1,0:T(8,128)S(1)}, f32[2,8,256]{2,1,0:T(8,128)S(1)}, u32[]{:S(2)}, u32[]{:S(2)}) collective-permute-start(f32[2,8,256]{2,1,0:T(8,128)S(1)} %get-tuple-element.216), channel_id=1, source_target_pairs={{0,127},{1,64},{2,65},{3,66},{4,67},{5,68},{6,69},{7,70},{8,71},{9... | collective-permute-start | bytes 49160 | tf_op jit(solution)/shard_map/ppermute | solution.py:581
  56.3 10.0 %conditional.5 = (f32[2,96,256]{2,1,0:T(8,128)}, f32[64,2,96,128]{3,2,1,0:T(8,128)S(1)}) conditional(s32[]{:T(128)} %bitcast.7, (f32[2,96,256]{2,1,0:T(8,128)S(1)}, f32[64,2,96,128]{3,2,1,0:T(8,128)S(1)}, bf16[64,32,256]{2,1,0:T(8,128)(2,1)S(1)}, f32[96,64,256]{2,1,0:T(8,128)}, f32[16,64,256]{2,1,0:T(8,128)}, ...), branch_computations={%region_6.7_spmd, %region_7.8_spmd, %region_8.9_spmd} | conditional | flops 4800000000 | bytes 14786488 | solution.py:593
  56.3 0.0 collective-permute-start.6
  56.3 9.7 %advance.9 = f32[64,2,96,128]{3,2,1,0:T(8,128)S(1)} custom-call(f32[64,2,96,128]{3,2,1,0:T(8,128)S(1)} %get-tuple-element.156.part, bf16[64,32,256]{2,1,0:T(8,128)(2,1)S(1)} %get-tuple-element.157.ghosts, f32[2,96,256]{2,1,0:T(8,128)S(1)} %get-tuple-element.155.faces, f32[96,64,256]{2,1,0:T(8,128)} %get-tuple-element.158.source, ...), custom_call_target="tpu_custom_call" | custom-call | flops 4800000000 | bytes 14000000 | tf_op jit(solution)/shard_map/cond/branch_0_fun/advance/pallas_call | solution.py:444
  66.3 6.5 %finish.1 = f32[96,64,256]{2,1,0:T(8,128)} custom-call(f32[5,64,256]{2,1,0:T(8,128)S(1)} %get-tuple-element.196.coef, f32[64,2,96,128]{3,2,1,0:T(8,128)S(1)} %get-tuple-element.213.part, f32[64,8,256]{2,1,0:T(8,128)S(1)} %collective-permute-done.15.plane, f32[2,8,256]{2,1,0:T(8,128)S(1)} %collective-permute-done.16.lo, ...), custom_call_target="tpu_custom_call" | custom-call | tf_op jit(solution)/shard_map/finish/pallas_call | solution.py:554
  (25 shorter events, 0.1 us)
Async XLA Ops:
  0.0 13.4 %copy-start.3 = (f32[1,1,6,6]{3,1,2,0:T(1,128)S(1)}, f32[1,1,6,6]{3,1,2,0:T(1,128)}, u32[]{:S(2)}) copy-start(f32[1,1,6,6]{3,1,2,0:T(1,128)} %param.21) | copy-start | bytes 436
  0.0 13.4 %copy-start.2 = (f32[1,1,64,4]{2,3,1,0:T(4,128)S(1)}, f32[1,1,64,4]{2,3,1,0:T(4,128)}, u32[]{:S(2)}) copy-start(f32[1,1,64,4]{2,3,1,0:T(4,128)} %param.24) | copy-start | bytes 3076
  0.0 13.4 %copy-start.1 = (s32[1,1,64,4]{2,3,1,0:T(4,128)S(1)}, s32[1,1,64,4]{2,3,1,0:T(4,128)}, u32[]{:S(2)}) copy-start(s32[1,1,64,4]{2,3,1,0:T(4,128)} %param.23) | copy-start | bytes 3076
  0.0 13.4 %copy-start = (f32[1,1,96,96]{3,2,1,0:T(8,128)S(1)}, f32[1,1,96,96]{3,2,1,0:T(8,128)}, u32[]{:S(2)}) copy-start(f32[1,1,96,96]{3,2,1,0:T(8,128)} %param.22) | copy-start | bytes 110596
  2.0 24.9 %collective-permute-start.9 = (f32[64,8,256]{2,1,0:T(8,128)S(1)}, f32[64,8,256]{2,1,0:T(8,128)S(1)}, u32[]{:S(2)}, u32[]{:S(2)}) collective-permute-start(f32[64,8,256]{2,1,0:T(8,128)S(1)} %get-tuple-element.200), channel_id=1, source_target_pairs={{0,64},{64,0},{1,65},{65,1},{2,66},{66,2},{3,67},{67,3},{4,68},{68... | collective-permute-start | bytes 1572872 | tf_op jit(solution)/shard_map/ppermute | solution.py:579
  3.5 23.4 %collective-permute-start.11 = (f32[2,8,256]{2,1,0:T(8,128)S(1)}, f32[2,8,256]{2,1,0:T(8,128)S(1)}, u32[]{:S(2)}, u32[]{:S(2)}) collective-permute-start(f32[2,8,256]{2,1,0:T(8,128)S(1)} %get-tuple-element.220), channel_id=1, source_target_pairs={{0,127},{1,64},{2,65},{3,66},{4,67},{5,68},{6,69},{7,70},{8,71},{9... | collective-permute-start | bytes 49160 | tf_op jit(solution)/shard_map/ppermute | solution.py:581
  12.0 14.9 %collective-permute-start.10 = (f32[2,8,256]{2,1,0:T(8,128)S(1)}, f32[2,8,256]{2,1,0:T(8,128)S(1)}, u32[]{:S(2)}, u32[]{:S(2)}) collective-permute-start(f32[2,8,256]{2,1,0:T(8,128)S(1)} %get-tuple-element.221), channel_id=1, source_target_pairs={{0,65},{1,66},{2,67},{3,68},{4,69},{5,70},{6,71},{7,72},{8,73},{9,... | collective-permute-start | bytes 49160 | tf_op jit(solution)/shard_map/ppermute | solution.py:580
  15.1 11.7 %collective-permute-start = (f32[2,96,256]{2,1,0:T(8,128)S(1)}, f32[2,96,256]{2,1,0:T(8,128)}, u32[]{:S(2)}, u32[]{:S(2)}) collective-permute-start(f32[2,96,256]{2,1,0:T(8,128)S(1)} %get-tuple-element.119), channel_id=1, source_target_pairs={{0,1},{1,0},{2,3},{3,2},{4,5},{5,4},{6,7},{7,6},{8,9},{9,8},{10,11... | collective-permute-start | bytes 589832 | tf_op jit(solution)/shard_map/cond/branch_0_fun/ppermute | solution.py:588
  29.1 17.6 %collective-permute-start.12 = (f32[64,8,256]{2,1,0:T(8,128)S(1)}, f32[64,8,256]{2,1,0:T(8,128)S(1)}, u32[]{:S(2)}, u32[]{:S(2)}) collective-permute-start(f32[64,8,256]{2,1,0:T(8,128)S(1)} %get-tuple-element.209), channel_id=1, source_target_pairs={{0,64},{64,0},{1,65},{65,1},{2,66},{66,2},{3,67},{67,3},{4,68},{68... | collective-permute-start | bytes 1572872 | tf_op jit(solution)/shard_map/ppermute | solution.py:579
  29.8 16.9 %collective-permute-start.14 = (f32[2,8,256]{2,1,0:T(8,128)S(1)}, f32[2,8,256]{2,1,0:T(8,128)S(1)}, u32[]{:S(2)}, u32[]{:S(2)}) collective-permute-start(f32[2,8,256]{2,1,0:T(8,128)S(1)} %get-tuple-element.218), channel_id=1, source_target_pairs={{0,127},{1,64},{2,65},{3,66},{4,67},{5,68},{6,69},{7,70},{8,71},{9... | collective-permute-start | bytes 49160 | tf_op jit(solution)/shard_map/ppermute | solution.py:581
  37.0 9.7 %collective-permute-start.13 = (f32[2,8,256]{2,1,0:T(8,128)S(1)}, f32[2,8,256]{2,1,0:T(8,128)S(1)}, u32[]{:S(2)}, u32[]{:S(2)}) collective-permute-start(f32[2,8,256]{2,1,0:T(8,128)S(1)} %get-tuple-element.219), channel_id=1, source_target_pairs={{0,65},{1,66},{2,67},{3,68},{4,69},{5,70},{6,71},{7,72},{8,73},{9,... | collective-permute-start | bytes 49160 | tf_op jit(solution)/shard_map/ppermute | solution.py:580
  37.0 9.7 %collective-permute-start.3 = (f32[2,96,256]{2,1,0:T(8,128)S(1)}, f32[2,96,256]{2,1,0:T(8,128)}, u32[]{:S(2)}, u32[]{:S(2)}) collective-permute-start(f32[2,96,256]{2,1,0:T(8,128)S(1)} %get-tuple-element.134.faces), channel_id=1, source_target_pairs={{0,1},{1,0},{2,3},{3,2},{4,5},{5,4},{6,7},{7,6},{8,9},{9,8},{10,11... | collective-permute-start | bytes 589832 | tf_op jit(solution)/shard_map/cond/branch_0_fun/ppermute | solution.py:588
  49.0 17.4 %collective-permute-start.15 = (f32[64,8,256]{2,1,0:T(8,128)S(1)}, f32[64,8,256]{2,1,0:T(8,128)S(1)}, u32[]{:S(2)}, u32[]{:S(2)}) collective-permute-start(f32[64,8,256]{2,1,0:T(8,128)S(1)} %get-tuple-element.214), channel_id=1, source_target_pairs={{0,64},{64,0},{1,65},{65,1},{2,66},{66,2},{3,67},{67,3},{4,68},{68... | collective-permute-start | bytes 1572872 | tf_op jit(solution)/shard_map/ppermute | solution.py:579
  49.1 17.2 %collective-permute-start.17 = (f32[2,8,256]{2,1,0:T(8,128)S(1)}, f32[2,8,256]{2,1,0:T(8,128)S(1)}, u32[]{:S(2)}, u32[]{:S(2)}) collective-permute-start(f32[2,8,256]{2,1,0:T(8,128)S(1)} %get-tuple-element.216), channel_id=1, source_target_pairs={{0,127},{1,64},{2,65},{3,66},{4,67},{5,68},{6,69},{7,70},{8,71},{9... | collective-permute-start | bytes 49160 | tf_op jit(solution)/shard_map/ppermute | solution.py:581
  56.3 10.0 %collective-permute-start.16 = (f32[2,8,256]{2,1,0:T(8,128)S(1)}, f32[2,8,256]{2,1,0:T(8,128)S(1)}, u32[]{:S(2)}, u32[]{:S(2)}) collective-permute-start(f32[2,8,256]{2,1,0:T(8,128)S(1)} %get-tuple-element.217), channel_id=1, source_target_pairs={{0,65},{1,66},{2,67},{3,68},{4,69},{5,70},{6,71},{7,72},{8,73},{9,... | collective-permute-start | bytes 49160 | tf_op jit(solution)/shard_map/ppermute | solution.py:580
  56.3 9.7 %collective-permute-start.6 = (f32[2,96,256]{2,1,0:T(8,128)S(1)}, f32[2,96,256]{2,1,0:T(8,128)}, u32[]{:S(2)}, u32[]{:S(2)}) collective-permute-start(f32[2,96,256]{2,1,0:T(8,128)S(1)} %get-tuple-element.155.faces), channel_id=1, source_target_pairs={{0,1},{1,0},{2,3},{3,2},{4,5},{5,4},{6,7},{7,6},{8,9},{9,8},{10,11... | collective-permute-start | bytes 589832 | tf_op jit(solution)/shard_map/cond/branch_0_fun/ppermute | solution.py:588

commit v4 on v3

--- a/solution.py
+++ b/solution.py
@@ -455,8 +455,10 @@
 
 def border_kernel(
     coef, edge, part, plane, lo, hi, faces, ghost_w, edge_w, face_w, flip_w,
-    ghosts, face_out, plane_out, window, stack, kept,
+    ghosts, face_out, plane_out, window, stack, kept, near, sem,
 ):
+    brought = pltpu.make_async_copy(faces, near, sem)
+    brought.start()
     fill_window(window, lo, hi, plane)
     at = edge[0]
 
@@ -474,8 +476,9 @@
         return carry
 
     lax.fori_loop(0, STEPS // 2, block, 0)
+    brought.wait()
     for side, j in ((0, 0), (1, NJ - 1)):
-        change = turned_face(faces.at[1 - side], stack, face_w, flip_w) + mul(ghost_w[...], ghosts[j])
+        change = turned_face(near.at[1 - side], stack, face_w, flip_w) + mul(ghost_w[...], ghosts[j])
         for h in range(2):
             kept[h] = part[j, h] + change[:, h * HALF : (h + 1) * HALF]
             face_out[side, :, lanes(h)] = kept[h]
@@ -491,12 +494,14 @@
             pltpu.VMEM((2, LN, NK), F32),
             pltpu.VMEM((NJ, 8, NK), F32),
         ],
-        in_specs=[VM, SM] + [VM] * 9,
+        in_specs=[VM, SM] + [VM] * 4 + [ANY] + [VM] * 4,
         out_specs=[VM] * 3,
         scratch_shapes=[
             pltpu.VMEM((NJ + 4, 8, NK), F32),
             pltpu.VMEM((2 * LN, NK), BF16),
             pltpu.VMEM((2, LN, HALF), F32),
+            pltpu.VMEM((2, LN, NK), F32),
+            pltpu.SemaphoreType.DMA(()),
         ],
         compiler_params=params(4),
         name="border",
@@ -504,9 +509,13 @@
 
 
 def finish_kernel(
-    coef, part, plane, lo, hi, faces, ghost_w, face_w, flip_w, out, window, stack, held, sems
+    coef, part, plane, lo, hi, faces, ghost_w, face_w, flip_w,
+    out, window, stack, held, sems, near, sem,
 ):
+    brought = pltpu.make_async_copy(faces, near, sem)
+    brought.start()
     fill_window(window, lo, hi, plane)
+    brought.wait()
 
     def copies(step, slot):
         rows = pl.ds(step * BLOCK, BLOCK)
@@ -520,8 +529,8 @@
             half = held.at[slot, h].reshape(LN * BLOCK, HALF)
             half[pl.ds(n, LN, stride=BLOCK), :] = part[j, h] + change[:, h * HALF : (h + 1) * HALF]
 
-    first = turned_face(faces.at[1], stack, face_w, flip_w)
-    last = turned_face(faces.at[0], stack, face_w, flip_w)
+    first = turned_face(near.at[1], stack, face_w, flip_w)
+    last = turned_face(near.at[0], stack, face_w, flip_w)
 
     def pair(step, carry):
         for slot in range(2):
@@ -554,13 +563,15 @@
     return pl.pallas_call(
         finish_kernel,
         out_shape=jax.ShapeDtypeStruct((LN, NJ, NK), F32),
-        in_specs=[VM] * 9,
+        in_specs=[VM] * 5 + [ANY] + [VM] * 3,
         out_specs=ANY,
         scratch_shapes=[
             pltpu.VMEM((NJ + 4, 8, NK), F32),
             pltpu.VMEM((2 * LN, NK), BF16),
             pltpu.VMEM((2, 2, LN, BLOCK, HALF), F32),
             pltpu.SemaphoreType.DMA((2, 2)),
+            pltpu.VMEM((2, LN, NK), F32),
+            pltpu.SemaphoreType.DMA(()),
         ],
         compiler_params=params(8),
         name="finish",

time: 73.6 us -> 72 us (0.978)
  Pallas kernels: 45.5 us -> 43.9 us
    pallas_call x2, Pallas kernels: 4.46 us -> 2.81 us  [border(): pl.pallas_call(border_kernel, out_shape=[pltpu.VMEM((NJ, 32, NK), BF16),...]
  transfers between devices with their start and end apart: 12 -> 12, of which waited for: 0 -> 0; matrix products, arithmetic and copies ran while one was open for 0% -> 0% of each run, Pallas kernels for 45% -> 46%
where the time goes in v4:
time: 72 us; the launch traced here: 71.4 us
  Pallas kernels  43.9 us (61%)
  starting transfers between devices  25.3 us (35%)
  between operations  1.71 us (2%)
    ppermute x3, starting transfers between devices, exchange(): hi = lax.ppermute(plane[:2], axes, across(-1))  22.8 us
    pallas_call x2, Pallas kernels, advance(): pl.pallas_call(advance_kernel, out_shape=pltpu.VMEM(PART, F32), in_specs=...  19.4 us
    pallas_call x1, Pallas kernels, interior(): pl.pallas_call(interior_kernel, out_shape=pltpu.VMEM(PART, F32), in_specs...  11.6 us
    pallas_call x1, Pallas kernels, finish(): pl.pallas_call(finish_kernel, out_shape=jax.ShapeDtypeStruct((LN, NJ, NK)...  6.47 us
    pallas_call x2, Pallas kernels, border(): pl.pallas_call(border_kernel, out_shape=[pltpu.VMEM((NJ, 32, NK), BF16),...  2.81 us
    ppermute x3, starting transfers between devices, exchange(): other = lax.ppermute(plane, 'row', [(0, 1), (1, 0)])  2.38 us
    pallas_call x1, Pallas kernels, begin(): pl.pallas_call(begin_kernel, out_shape=[pltpu.VMEM((2, LN, NK), F32), plt...  1.95 us
    pallas_call x1, Pallas kernels, prepare(): pl.pallas_call(prepare_kernel, out_shape=[pltpu.VMEM((2 * LN, 4 * LN), BF...  1.64 us
  transfers between devices with their start and end apart: 12, of which 0 were waited for; matrix products, arithmetic and copies ran while one was open for 0% of the time, Pallas kernels for 46%

profile of v4, /device:TPU:1, one launch (start us, length us, event | category | flops | bytes accessed | tf_op | source)
XLA Modules:
  0.0 71.4 jit_solution(7533365472188293771)
XLA Ops:
  0.0 1.9 %begin.1 = (f32[2,96,256]{2,1,0:T(8,128)S(1)}, f32[64,8,256]{2,1,0:T(8,128)S(1)}) custom-call(s32[1]{0:T(128)} %bitcast.8.edge, f32[96,64,256]{2,1,0:T(8,128)} %bitcast.22), custom_call_target="tpu_custom_call" | custom-call | tf_op jit(solution)/shard_map/begin/pallas_call | solution.py:172
  2.0 1.5 %collective-permute-start.9 = (f32[64,8,256]{2,1,0:T(8,128)S(1)}, f32[64,8,256]{2,1,0:T(8,128)S(1)}, u32[]{:S(2)}, u32[]{:S(2)}) collective-permute-start(f32[64,8,256]{2,1,0:T(8,128)S(1)} %get-tuple-element.200), channel_id=1, source_target_pairs={{0,64},{64,0},{1,65},{65,1},{2,66},{66,2},{3,67},{67,3},{4,68},{68... | collective-permute-start | bytes 1572872 | tf_op jit(solution)/shard_map/ppermute | solution.py:590
  3.5 8.5 %collective-permute-start.11 = (f32[2,8,256]{2,1,0:T(8,128)S(1)}, f32[2,8,256]{2,1,0:T(8,128)S(1)}, u32[]{:S(2)}, u32[]{:S(2)}) collective-permute-start(f32[2,8,256]{2,1,0:T(8,128)S(1)} %get-tuple-element.220), channel_id=1, source_target_pairs={{0,127},{1,64},{2,65},{3,66},{4,67},{5,68},{6,69},{7,70},{8,71},{9... | collective-permute-start | bytes 49160 | tf_op jit(solution)/shard_map/ppermute | solution.py:592
  12.0 0.0 collective-permute-start.10
  12.6 0.1 pad_add_fusion.flags
  13.4 1.6 %prepare.1 = (bf16[192,384]{1,0:T(8,128)(2,1)S(1)}, bf16[96,32]{1,0:T(8,128)(2,1)S(1)}, bf16[16,32]{1,0:T(8,128)(2,1)S(1)}, bf16[192,192]{1,0:T(8,128)(2,1)S(1)}...) custom-call(s32[2]{0:T(128)S(1)} %pad_add_fusion.flags, f32[96,96]{1,0:T(8,128)S(1)} %bitcast.19, ...), custom_call_target="tpu_custom_call" | custom-call | tf_op jit(solution)/shard_map/prepare/pallas_call | solution.py:125
  15.1 11.8 %conditional.3 = (f32[2,96,256]{2,1,0:T(8,128)}, f32[64,2,96,128]{3,2,1,0:T(8,128)S(1)}) conditional(s32[]{:T(128)} %bitcast.7, (f32[2,96,256]{2,1,0:T(8,128)S(1)}, f32[96,64,256]{2,1,0:T(8,128)}, f32[96,64,256]{2,1,0:T(8,128)}, f32[16,64,256]{2,1,0:T(8,128)}, bf16[192,384]{1,0:T(8,128)(2,1)S(1)}) %tuple.59, ...), branch_computations={%region_0.1_spmd, %region_1.2_spmd, %region_2.3_spmd} | conditional | flops 4800000000 | bytes 14786488 | solution.py:604
  15.1 0.1 collective-permute-start
  15.2 11.6 %interior.3 = f32[64,2,96,128]{3,2,1,0:T(8,128)S(1)} custom-call(f32[96,64,256]{2,1,0:T(8,128)} %get-tuple-element.120.state, f32[96,64,256]{2,1,0:T(8,128)} %get-tuple-element.121.source, f32[16,64,256]{2,1,0:T(8,128)} %get-tuple-element.122.diagonal, bf16[192,384]{1,0:T(8,128)(2,1)S(1)} %get-tuple-element.123.weights), custom_call_target="tpu_custom_call" | custom-call | flops 4800000000 | bytes 14000000 | tf_op jit(solution)/shard_map/cond/branch_0_fun/interior/pallas_call | solution.py:364
  26.8 0.0 collective-permute-done
  26.8 0.0 collective-permute-done.11.hi
  26.9 0.0 collective-permute-done.10.lo
  26.9 1.4 %border.2 = (bf16[64,32,256]{2,1,0:T(8,128)(2,1)S(1)}, f32[2,96,256]{2,1,0:T(8,128)S(1)}, f32[64,8,256]{2,1,0:T(8,128)S(1)}) custom-call(f32[5,64,256]{2,1,0:T(8,128)S(1)} %get-tuple-element.196.coef, s32[1]{0:T(128)} %bitcast.8.edge, f32[64,2,96,128]{3,2,1,0:T(8,128)S(1)} %get-tuple-element.199.part, f32[64,8,256]{2,1,0:T(8,128)S(1)} %collective-permute-done.9.plane, ...), custom_call_target="tpu_custom_call" | custom-call | tf_op jit(solution)/shard_map/border/pallas_call | solution.py:490
  28.3 0.7 collective-permute-start.12
  29.0 7.2 %collective-permute-start.14 = (f32[2,8,256]{2,1,0:T(8,128)S(1)}, f32[2,8,256]{2,1,0:T(8,128)S(1)}, u32[]{:S(2)}, u32[]{:S(2)}) collective-permute-start(f32[2,8,256]{2,1,0:T(8,128)S(1)} %get-tuple-element.218), channel_id=1, source_target_pairs={{0,127},{1,64},{2,65},{3,66},{4,67},{5,68},{6,69},{7,70},{8,71},{9... | collective-permute-start | bytes 49160 | tf_op jit(solution)/shard_map/ppermute | solution.py:592
  36.2 9.7 %conditional.4 = (f32[2,96,256]{2,1,0:T(8,128)}, f32[64,2,96,128]{3,2,1,0:T(8,128)S(1)}) conditional(s32[]{:T(128)} %bitcast.7, (f32[2,96,256]{2,1,0:T(8,128)S(1)}, f32[64,2,96,128]{3,2,1,0:T(8,128)S(1)}, bf16[64,32,256]{2,1,0:T(8,128)(2,1)S(1)}, f32[96,64,256]{2,1,0:T(8,128)}, f32[16,64,256]{2,1,0:T(8,128)}, ...), branch_computations={%region_3.4_spmd, %region_4.5_spmd, %region_5.6_spmd} | conditional | flops 4800000000 | bytes 14786488 | solution.py:604
  36.2 9.7 %advance.6 = f32[64,2,96,128]{3,2,1,0:T(8,128)S(1)} custom-call(f32[64,2,96,128]{3,2,1,0:T(8,128)S(1)} %get-tuple-element.135.part, bf16[64,32,256]{2,1,0:T(8,128)(2,1)S(1)} %get-tuple-element.136.ghosts, f32[2,96,256]{2,1,0:T(8,128)S(1)} %get-tuple-element.134.faces, f32[96,64,256]{2,1,0:T(8,128)} %get-tuple-element.137.source, ...), custom_call_target="tpu_custom_call" | custom-call | flops 4800000000 | bytes 14000000 | tf_op jit(solution)/shard_map/cond/branch_0_fun/advance/pallas_call | solution.py:444
  45.9 1.4 %border.3 = (bf16[64,32,256]{2,1,0:T(8,128)(2,1)S(1)}, f32[2,96,256]{2,1,0:T(8,128)S(1)}, f32[64,8,256]{2,1,0:T(8,128)S(1)}) custom-call(f32[5,64,256]{2,1,0:T(8,128)S(1)} %get-tuple-element.196.coef, s32[1]{0:T(128)} %bitcast.8.edge, f32[64,2,96,128]{3,2,1,0:T(8,128)S(1)} %get-tuple-element.208.part, f32[64,8,256]{2,1,0:T(8,128)S(1)} %collective-permute-done.12.plane, ...), custom_call_target="tpu_custom_call" | custom-call | tf_op jit(solution)/shard_map/border/pallas_call | solution.py:490
  47.3 0.2 collective-permute-start.15
  47.5 7.2 %collective-permute-start.17 = (f32[2,8,256]{2,1,0:T(8,128)S(1)}, f32[2,8,256]{2,1,0:T(8,128)S(1)}, u32[]{:S(2)}, u32[]{:S(2)}) collective-permute-start(f32[2,8,256]{2,1,0:T(8,128)S(1)} %get-tuple-element.216), channel_id=1, source_target_pairs={{0,127},{1,64},{2,65},{3,66},{4,67},{5,68},{6,69},{7,70},{8,71},{9... | collective-permute-start | bytes 49160 | tf_op jit(solution)/shard_map/ppermute | solution.py:592
  54.7 10.0 %conditional.5 = (f32[2,96,256]{2,1,0:T(8,128)}, f32[64,2,96,128]{3,2,1,0:T(8,128)S(1)}) conditional(s32[]{:T(128)} %bitcast.7, (f32[2,96,256]{2,1,0:T(8,128)S(1)}, f32[64,2,96,128]{3,2,1,0:T(8,128)S(1)}, bf16[64,32,256]{2,1,0:T(8,128)(2,1)S(1)}, f32[96,64,256]{2,1,0:T(8,128)}, f32[16,64,256]{2,1,0:T(8,128)}, ...), branch_computations={%region_6.7_spmd, %region_7.8_spmd, %region_8.9_spmd} | conditional | flops 4800000000 | bytes 14786488 | solution.py:604
  54.7 0.0 collective-permute-start.6
  54.7 9.7 %advance.9 = f32[64,2,96,128]{3,2,1,0:T(8,128)S(1)} custom-call(f32[64,2,96,128]{3,2,1,0:T(8,128)S(1)} %get-tuple-element.156.part, bf16[64,32,256]{2,1,0:T(8,128)(2,1)S(1)} %get-tuple-element.157.ghosts, f32[2,96,256]{2,1,0:T(8,128)S(1)} %get-tuple-element.155.faces, f32[96,64,256]{2,1,0:T(8,128)} %get-tuple-element.158.source, ...), custom_call_target="tpu_custom_call" | custom-call | flops 4800000000 | bytes 14000000 | tf_op jit(solution)/shard_map/cond/branch_0_fun/advance/pallas_call | solution.py:444
  64.7 6.5 %finish.1 = f32[96,64,256]{2,1,0:T(8,128)} custom-call(f32[5,64,256]{2,1,0:T(8,128)S(1)} %get-tuple-element.196.coef, f32[64,2,96,128]{3,2,1,0:T(8,128)S(1)} %get-tuple-element.213.part, f32[64,8,256]{2,1,0:T(8,128)S(1)} %collective-permute-done.15.plane, f32[2,8,256]{2,1,0:T(8,128)S(1)} %collective-permute-done.16.lo, ...), custom_call_target="tpu_custom_call" | custom-call | tf_op jit(solution)/shard_map/finish/pallas_call | solution.py:563
  (25 shorter events, 0.1 us)
Async XLA Ops:
  0.0 13.4 %copy-start.3 = (f32[1,1,6,6]{3,1,2,0:T(1,128)S(1)}, f32[1,1,6,6]{3,1,2,0:T(1,128)}, u32[]{:S(2)}) copy-start(f32[1,1,6,6]{3,1,2,0:T(1,128)} %param.21) | copy-start | bytes 436
  0.0 13.4 %copy-start.2 = (f32[1,1,64,4]{2,3,1,0:T(4,128)S(1)}, f32[1,1,64,4]{2,3,1,0:T(4,128)}, u32[]{:S(2)}) copy-start(f32[1,1,64,4]{2,3,1,0:T(4,128)} %param.24) | copy-start | bytes 3076
  0.0 13.4 %copy-start.1 = (s32[1,1,64,4]{2,3,1,0:T(4,128)S(1)}, s32[1,1,64,4]{2,3,1,0:T(4,128)}, u32[]{:S(2)}) copy-start(s32[1,1,64,4]{2,3,1,0:T(4,128)} %param.23) | copy-start | bytes 3076
  0.0 13.4 %copy-start = (f32[1,1,96,96]{3,2,1,0:T(8,128)S(1)}, f32[1,1,96,96]{3,2,1,0:T(8,128)}, u32[]{:S(2)}) copy-start(f32[1,1,96,96]{3,2,1,0:T(8,128)} %param.22) | copy-start | bytes 110596
  2.0 24.9 %collective-permute-start.9 = (f32[64,8,256]{2,1,0:T(8,128)S(1)}, f32[64,8,256]{2,1,0:T(8,128)S(1)}, u32[]{:S(2)}, u32[]{:S(2)}) collective-permute-start(f32[64,8,256]{2,1,0:T(8,128)S(1)} %get-tuple-element.200), channel_id=1, source_target_pairs={{0,64},{64,0},{1,65},{65,1},{2,66},{66,2},{3,67},{67,3},{4,68},{68... | collective-permute-start | bytes 1572872 | tf_op jit(solution)/shard_map/ppermute | solution.py:590
  3.5 23.4 %collective-permute-start.11 = (f32[2,8,256]{2,1,0:T(8,128)S(1)}, f32[2,8,256]{2,1,0:T(8,128)S(1)}, u32[]{:S(2)}, u32[]{:S(2)}) collective-permute-start(f32[2,8,256]{2,1,0:T(8,128)S(1)} %get-tuple-element.220), channel_id=1, source_target_pairs={{0,127},{1,64},{2,65},{3,66},{4,67},{5,68},{6,69},{7,70},{8,71},{9... | collective-permute-start | bytes 49160 | tf_op jit(solution)/shard_map/ppermute | solution.py:592
  12.0 14.9 %collective-permute-start.10 = (f32[2,8,256]{2,1,0:T(8,128)S(1)}, f32[2,8,256]{2,1,0:T(8,128)S(1)}, u32[]{:S(2)}, u32[]{:S(2)}) collective-permute-start(f32[2,8,256]{2,1,0:T(8,128)S(1)} %get-tuple-element.221), channel_id=1, source_target_pairs={{0,65},{1,66},{2,67},{3,68},{4,69},{5,70},{6,71},{7,72},{8,73},{9,... | collective-permute-start | bytes 49160 | tf_op jit(solution)/shard_map/ppermute | solution.py:591
  15.1 11.7 %collective-permute-start = (f32[2,96,256]{2,1,0:T(8,128)S(1)}, f32[2,96,256]{2,1,0:T(8,128)}, u32[]{:S(2)}, u32[]{:S(2)}) collective-permute-start(f32[2,96,256]{2,1,0:T(8,128)S(1)} %get-tuple-element.119), channel_id=1, source_target_pairs={{0,1},{1,0},{2,3},{3,2},{4,5},{5,4},{6,7},{7,6},{8,9},{9,8},{10,11... | collective-permute-start | bytes 589832 | tf_op jit(solution)/shard_map/cond/branch_0_fun/ppermute | solution.py:599
  28.3 17.6 %collective-permute-start.12 = (f32[64,8,256]{2,1,0:T(8,128)S(1)}, f32[64,8,256]{2,1,0:T(8,128)S(1)}, u32[]{:S(2)}, u32[]{:S(2)}) collective-permute-start(f32[64,8,256]{2,1,0:T(8,128)S(1)} %get-tuple-element.209), channel_id=1, source_target_pairs={{0,64},{64,0},{1,65},{65,1},{2,66},{66,2},{3,67},{67,3},{4,68},{68... | collective-permute-start | bytes 1572872 | tf_op jit(solution)/shard_map/ppermute | solution.py:590
  29.0 16.9 %collective-permute-start.14 = (f32[2,8,256]{2,1,0:T(8,128)S(1)}, f32[2,8,256]{2,1,0:T(8,128)S(1)}, u32[]{:S(2)}, u32[]{:S(2)}) collective-permute-start(f32[2,8,256]{2,1,0:T(8,128)S(1)} %get-tuple-element.218), channel_id=1, source_target_pairs={{0,127},{1,64},{2,65},{3,66},{4,67},{5,68},{6,69},{7,70},{8,71},{9... | collective-permute-start | bytes 49160 | tf_op jit(solution)/shard_map/ppermute | solution.py:592
  36.2 9.7 %collective-permute-start.13 = (f32[2,8,256]{2,1,0:T(8,128)S(1)}, f32[2,8,256]{2,1,0:T(8,128)S(1)}, u32[]{:S(2)}, u32[]{:S(2)}) collective-permute-start(f32[2,8,256]{2,1,0:T(8,128)S(1)} %get-tuple-element.219), channel_id=1, source_target_pairs={{0,65},{1,66},{2,67},{3,68},{4,69},{5,70},{6,71},{7,72},{8,73},{9,... | collective-permute-start | bytes 49160 | tf_op jit(solution)/shard_map/ppermute | solution.py:591
  36.2 9.7 %collective-permute-start.3 = (f32[2,96,256]{2,1,0:T(8,128)S(1)}, f32[2,96,256]{2,1,0:T(8,128)}, u32[]{:S(2)}, u32[]{:S(2)}) collective-permute-start(f32[2,96,256]{2,1,0:T(8,128)S(1)} %get-tuple-element.134.faces), channel_id=1, source_target_pairs={{0,1},{1,0},{2,3},{3,2},{4,5},{5,4},{6,7},{7,6},{8,9},{9,8},{10,11... | collective-permute-start | bytes 589832 | tf_op jit(solution)/shard_map/cond/branch_0_fun/ppermute | solution.py:599
  47.3 17.4 %collective-permute-start.15 = (f32[64,8,256]{2,1,0:T(8,128)S(1)}, f32[64,8,256]{2,1,0:T(8,128)S(1)}, u32[]{:S(2)}, u32[]{:S(2)}) collective-permute-start(f32[64,8,256]{2,1,0:T(8,128)S(1)} %get-tuple-element.214), channel_id=1, source_target_pairs={{0,64},{64,0},{1,65},{65,1},{2,66},{66,2},{3,67},{67,3},{4,68},{68... | collective-permute-start | bytes 1572872 | tf_op jit(solution)/shard_map/ppermute | solution.py:590
  47.5 17.2 %collective-permute-start.17 = (f32[2,8,256]{2,1,0:T(8,128)S(1)}, f32[2,8,256]{2,1,0:T(8,128)S(1)}, u32[]{:S(2)}, u32[]{:S(2)}) collective-permute-start(f32[2,8,256]{2,1,0:T(8,128)S(1)} %get-tuple-element.216), channel_id=1, source_target_pairs={{0,127},{1,64},{2,65},{3,66},{4,67},{5,68},{6,69},{7,70},{8,71},{9... | collective-permute-start | bytes 49160 | tf_op jit(solution)/shard_map/ppermute | solution.py:592
  54.7 10.0 %collective-permute-start.16 = (f32[2,8,256]{2,1,0:T(8,128)S(1)}, f32[2,8,256]{2,1,0:T(8,128)S(1)}, u32[]{:S(2)}, u32[]{:S(2)}) collective-permute-start(f32[2,8,256]{2,1,0:T(8,128)S(1)} %get-tuple-element.217), channel_id=1, source_target_pairs={{0,65},{1,66},{2,67},{3,68},{4,69},{5,70},{6,71},{7,72},{8,73},{9,... | collective-permute-start | bytes 49160 | tf_op jit(solution)/shard_map/ppermute | solution.py:591
  54.7 9.7 %collective-permute-start.6 = (f32[2,96,256]{2,1,0:T(8,128)S(1)}, f32[2,96,256]{2,1,0:T(8,128)}, u32[]{:S(2)}, u32[]{:S(2)}) collective-permute-start(f32[2,96,256]{2,1,0:T(8,128)S(1)} %get-tuple-element.155.faces), channel_id=1, source_target_pairs={{0,1},{1,0},{2,3},{3,2},{4,5},{5,4},{6,7},{7,6},{8,9},{9,8},{10,11... | collective-permute-start | bytes 589832 | tf_op jit(solution)/shard_map/cond/branch_0_fun/ppermute | solution.py:599
